TPU v7x, 256 devices: a whole 4x4x8 slice. The times are simulated.
256 devices in a mesh: dp: 16 (over z, core), tensor: 8 (over y, x_hi), mp: 2 (over x_lo).
Axes of the slice: x: 4 (x_hi: 2, x_lo: 2; x = x_hi * 2 + x_lo), y: 4, z: 8, core: 2. Of those that a mesh axis runs over, the one named last changes fastest.
Arguments:
- step_embeds: bfloat16 [2, 512, 32, 8192], P('mp', 'dp', None, 'tensor'), may hold values from -6 to 6
- step_len: int32 [512], replicated, may hold values from 8 to 32, as said below
- leaf_of_step: int32 [512], replicated, may hold values from 0 to 63, as said below
- cache_len: int32 [64], P('dp'), may hold values from 96 to 768, as said below
- caches: bfloat16 [2, 64, 768, 2048], P('mp', 'dp', None, 'tensor'), may hold values from -500 to 500
- norm_gain: float32 [2, 8192], P('mp'), may hold values from 0.1 to 1.9
- qkv_weight: bfloat16 [2, 8192, 6144], P('mp', 'dp', 'tensor'), may hold values from -0.1875 to 0.1875
- score_weight: float32 [2, 4096], P('mp', 'tensor'), may hold values from -0.09375 to 0.09375
Outputs:
- contexts: bfloat16 [2, 64, 8, 32, 4096], P('mp', 'dp', None, None, 'tensor')
- step_value: float32 [64, 8], P('dp')
Inputs may be any that keep to these rules, and one draw needn't show every extreme that they name: `leaf_of_step`: every leaf is named by exactly 8 steps, and each aligned block of 32 steps names the leaves of every aligned block of 4 leaves equally often. `step_len`: some step has all 32 tokens. `cache_len`: some leaf fills all 768 cache positions.
All inputs are finite; a program needn't handle non-finite values.
Results may differ from a plain program's by a relative error of at most 0.0049.
The roundings to bfloat16 on the way count: a program that leaves them out, or rounds other values in their place, can miss the bound.
Values may be sent and summed in bfloat16 or wider, within the bound.
No kernel may reach another device: no remote copies, remote signals or barrier semaphores. Data moves between devices by JAX's collectives and lax.ppermute only.
A program may use at most 192 MiB of HBM per device.

v0:
```python
import jax
import jax.numpy as jnp
from jax import lax
from jax.sharding import PartitionSpec as P

KVH = 8
HD = 128
HQ = 32


prior_weight = 0.5
norm_eps = 1e-05
key_block = 256


def sent_to_all(value, axis):
    length = lax.axis_size(axis)
    return lax.all_to_all(
        jnp.broadcast_to(value[None], (length, *value.shape)), axis, 0, 0, tiled=True
    )


def taken_together(value, axis):
    everything = sent_to_all(value, axis)
    return jnp.sum(everything, axis=0)


def per_device(
    step_embeds, step_len, leaf_of_step, cache_len, caches, norm_gain, qkv_weight, score_weight
):
    embeds = step_embeds[0]
    steps_here, seq_max, piece_width = embeds.shape
    row_width = norm_gain.shape[1]
    leaves_here = cache_len.shape[0]
    per_leaf = steps_here // leaves_here
    groups = caches.shape[3] // (2 * HD)
    group_size = HQ // KVH
    part_count = lax.axis_size("dp")
    dp_index = lax.axis_index("dp")
    per_peer = steps_here // part_count
    total_steps = leaf_of_step.shape[0]
    local_ids = jnp.arange(steps_here, dtype=jnp.int32)
    owners = (leaf_of_step // leaves_here).reshape(part_count, steps_here)
    send_orders = jnp.argsort(owners * steps_here + local_ids[None, :], axis=1)
    send_order = lax.dynamic_index_in_dim(send_orders, dp_index, 0, keepdims=False)
    sources = jnp.arange(part_count, dtype=jnp.int32)[:, None] * steps_here
    arriving = (
        lax.dynamic_slice_in_dim(send_orders, dp_index * per_peer, per_peer, 1) + sources
    ).reshape(steps_here)
    arrive_leaf = leaf_of_step[arriving] - dp_index * leaves_here
    arrange = jnp.argsort(arrive_leaf * total_steps + arriving)
    step_ids = arriving[arrange]
    lengths = step_len[step_ids].reshape(leaves_here, per_leaf)
    outgoing = embeds[send_order]
    local_rows = lax.all_gather(outgoing, "tensor", axis=2, tiled=True)
    as_float = local_rows.reshape(steps_here * seq_max, row_width).astype(jnp.float32)
    inverse_rms = lax.rsqrt(jnp.mean(as_float * as_float, axis=-1, keepdims=True) + norm_eps)
    normed = (as_float * inverse_rms * norm_gain[0]).astype(jnp.bfloat16)
    summed = jnp.dot(
        normed,
        lax.all_gather(qkv_weight[0], "dp", axis=0, tiled=True),
        preferred_element_type=jnp.float32,
    )
    outbound = summed.astype(jnp.bfloat16)
    outbound = outbound.reshape(part_count, per_peer, seq_max, outbound.shape[-1])
    arrived = lax.all_to_all(outbound, "dp", split_axis=0, concat_axis=0, tiled=True)
    projected = arrived.reshape(steps_here, seq_max, arrived.shape[-1])[arrange]
    projected = projected.reshape(leaves_here, per_leaf, seq_max, groups, group_size + 2, HD)
    queries = projected[:, :, :, :, :group_size]
    key_own = projected[:, :, :, :, group_size]
    value_own = projected[:, :, :, :, group_size + 1]
    scale_q = HD ** (-0.5)
    own_scores = (
        jnp.einsum("lsikgh,lsjkh->lsikgj", queries, key_own, preferred_element_type=jnp.float32)
        * scale_q
    )
    positions = jnp.arange(seq_max, dtype=jnp.int32)
    causal = positions[None, :] <= positions[:, None]
    own_scores = jnp.where(causal[:, None, None, :], own_scores, -jnp.inf)
    running_max = own_scores.max(-1)
    weights = jnp.exp(own_scores - running_max[..., None])
    running_sum = weights.sum(-1)
    weighted = jnp.einsum(
        "lsikgj,lsjkh->lsikgh",
        weights.astype(jnp.bfloat16),
        value_own,
        preferred_element_type=jnp.float32,
    )
    cache_rows = caches[0].reshape(leaves_here, caches.shape[2], groups, 2, HD)

    def visit(block_index, carry):
        old_max, old_sum, old_weighted = carry
        block_start = block_index * key_block
        block_rows = lax.dynamic_slice_in_dim(cache_rows, block_start, key_block, 1)
        block_keys = block_rows[:, :, :, 0]
        block_values = block_rows[:, :, :, 1]
        scores = (
            jnp.einsum(
                "lsikgh,lckh->lsikgc", queries, block_keys, preferred_element_type=jnp.float32
            )
            * scale_q
        )
        is_live = (block_start + jnp.arange(key_block, dtype=jnp.int32))[None, :] < cache_len[
            :, None
        ]
        scores = jnp.where(is_live[:, None, None, None, None, :], scores, -jnp.inf)
        new_max = jnp.maximum(old_max, scores.max(-1))
        rescale = jnp.exp(old_max - new_max)
        block_weights = jnp.exp(scores - new_max[..., None])
        new_sum = old_sum * rescale + block_weights.sum(-1)
        new_weighted = old_weighted * rescale[..., None] + jnp.einsum(
            "lsikgc,lckh->lsikgh",
            block_weights.astype(jnp.bfloat16),
            block_values,
            preferred_element_type=jnp.float32,
        )
        return (new_max, new_sum, new_weighted)

    block_count = (jnp.max(cache_len) + key_block - 1) // key_block
    running_max, running_sum, weighted = lax.fori_loop(
        0, block_count, visit, (running_max, running_sum, weighted)
    )
    context = weighted / running_sum[..., None]
    is_valid = positions[None, None, :] < lengths[:, :, None]
    context = jnp.where(is_valid[:, :, :, None, None, None], context, 0.0)
    flat = context.reshape(leaves_here, per_leaf, seq_max, groups * group_size * HD)
    contexts = flat.astype(jnp.bfloat16)[None]
    last_token = (positions[None, None, :] == lengths[:, :, None] - 1).astype(jnp.float32)
    last_context = jnp.sum(last_token[:, :, :, None] * flat, axis=2)
    partial_value = jnp.sum(last_context * score_weight[0], axis=-1)
    model_weight = jnp.where(lax.axis_index("mp") == 0, prior_weight, 1.0).astype(jnp.float32)
    step_value = taken_together(partial_value * model_weight, ("tensor", "mp"))
    return (contexts, step_value)


def solution(mesh):
    placed = (
        P("mp", "dp", None, "tensor"),
        P(),
        P(),
        P("dp"),
        P("mp", "dp", None, "tensor"),
        P("mp", None),
        P("mp", "dp", "tensor"),
        P("mp", "tensor"),
    )
    return jax.shard_map(
        per_device,
        mesh=mesh,
        in_specs=placed,
        out_specs=(P("mp", "dp", None, None, "tensor"), P("dp", None)),
        check_vma=False,
    )
```

profile of v0, /device:TPU:1, one launch (start us, length us, event | category | flops | bytes accessed | tf_op | source)
XLA Modules:
  0.0 403.8 jit_solution(6394626255613146861)
XLA Ops:
  9.5 2.0 gather_fusion.3
  12.3 189.7 %all-gather.5.cloned.1.call-done = bf16[32,32,8192]{2,1,0:T(8,128)(2,1)} async-done(((bf16[32,32,1024]{2,1,0:T(8,128)(2,1)}), bf16[32,32,8192]{2,1,0:T(8,128)(2,1)}) %all-gather.5.cloned.1.call-update) | async-done | bytes 16777232 | tf_op jit(solution)/shard_map/all_gather | solution.py:55
  202.0 7.3 %multiply_reduce_fusion = f32[32,32]{1,0:T(8,128)S(1)} fusion(bf16[32,32,8192]{2,1,0:T(8,128)(2,1)} %all-gather.5.cloned.1.call-done), kind=kLoop, calls=%fused_computation.35 | loop fusion | flops 25164800 | bytes 16781312 | tf_op jit(solution)/shard_map/reduce_sum | solution.py:57
  209.3 15.4 %fusion.20 = bf16[1024,8192]{1,0:T(8,128)(2,1)} fusion(f32[8192]{0:T(1024)S(1)} %bitcast.171, f32[1024]{0:T(1024)S(1)} %rsqrt.12, bf16[32,32,8192]{2,1,0:T(8,128)(2,1)} %all-gather.5.cloned.1.call-done), kind=kLoop, calls=%fused_computation.34 | loop fusion | flops 33554432 | bytes 33591296 | tf_op jit(solution)/shard_map/convert_element_type | solution.py:58
  224.7 53.8 %all-gather.7.cloned.1.call-done = bf16[1,8192,768]{2,1,0:T(8,128)(2,1)} async-done(((bf16[1,512,768]{2,1,0:T(8,128)(2,1)}), bf16[1,8192,768]{2,1,0:T(8,128)(2,1)}) %all-gather.7.cloned.1.call-update) | async-done | bytes 12582928 | tf_op jit(solution)/shard_map/all_gather | solution.py:61
  278.5 19.8 %fusion.25 = bf16[1024,768]{1,0:T(8,128)(2,1)} fusion(bf16[1024,8192]{1,0:T(8,128)(2,1)} %fusion.20, bf16[1,8192,768]{2,1,0:T(8,128)(2,1)} %all-gather.7.cloned.1.call-done), kind=kOutput, calls=%fused_computation.44 | convolution fusion | flops 12885688320 | bytes 30932992 | tf_op jit(solution)/shard_map/dot_general | solution.py:59
  298.4 4.7 %all-to-all-start = ((bf16[16,2,32,768]{3,2,1,0:T(8,128)(2,1)}), bf16[16,2,32,768]{3,2,1,0:T(8,128)(2,1)S(1)}, u32[]{:S(2)}, u32[]{:S(2)}) async-start(bf16[16,2,32,768]{3,2,1,0:T(8,128)(2,1)} %bitcast.170), calls=%async_computation | async-start | bytes 3145728 | tf_op jit(solution)/shard_map/all_to_all | solution.py:66
  305.2 2.6 copy.48
  307.8 1.6 sort.35
  311.1 30.5 %all-to-all-done = bf16[16,2,32,768]{3,2,1,0:T(8,128)(2,1)S(1)} async-done(((bf16[16,2,32,768]{3,2,1,0:T(8,128)(2,1)}), bf16[16,2,32,768]{3,2,1,0:T(8,128)(2,1)S(1)}, u32[]{:S(2)}, u32[]{:S(2)}) %all-to-all-start) | async-done | bytes 1572896 | tf_op jit(solution)/shard_map/all_to_all | solution.py:66
  341.6 1.8 gather_fusion.4
  343.4 3.4 reshape.237
  349.3 2.0 slice.29
  351.6 1.8 fusion.42
  354.6 26.7 %while.14 = (s32[]{:T(128)}, f32[4,8,32,1,4]{2,4,1,0,3:T(4,128)S(1)}, f32[4,8,32,1,4]{2,4,1,0,3:T(4,128)S(1)}, f32[4,8,32,1,4,128]{5,2,4,1,0,3:T(8,128)S(1)}, s3...) while((s32[]{:T(128)}, ...), condition=%wide.region_9.10_spmd, body=%wide.region_6.9_spmd.sunk | while | flops 549467392 | bytes 35395824 | solution.py:120
  354.7 3.6 bitcast_reduce_fusion.2
  358.4 3.5 bitcast_add_fusion.5
  363.6 3.6 bitcast_reduce_fusion.2
  367.3 3.5 bitcast_add_fusion.5
  372.5 3.6 bitcast_reduce_fusion.2
  376.2 3.5 bitcast_add_fusion.5
  383.2 6.5 %all-to-all-start.1 = ((f32[16,4,8]{2,1,0:T(4,128)}), f32[16,4,8]{2,1,0:T(4,128)S(1)}, u32[]{:S(2)}, u32[]{:S(2)}) async-start(f32[16,4,8]{2,1,0:T(4,128)} %broadcast_in_dim.50), calls=%async_computation.1 | async-start | bytes 65536 | tf_op jit(solution)/shard_map/all_to_all | solution.py:18
  391.3 2.2 convert_element_type.48
  393.5 2.8 all-to-all-done.1
  (86 shorter events, 19.5 us)
Async XLA Ops:
  7.2 2.3 copy-start
  7.2 194.8 %all-gather.5.cloned.1.call-start = ((), (), s32[]{:S(2)}) async-start(), calls=%async_computation.2 | async-start | bytes 18874368 | tf_op jit(solution)/shard_map/all_gather | solution.py:55
  11.5 267.0 %all-gather.7.cloned.1.call-start = ((), (), s32[]{:S(2)}) async-start(), calls=%async_computation.3 | async-start | bytes 13369344 | tf_op jit(solution)/shard_map/all_gather | solution.py:61
  12.3 197.1 %copy-start.6 = (f32[1,8192]{1,0:T(1,128)S(1)}, f32[1,8192]{1,0:T(1,128)}, u32[]{:S(2)}) copy-start(f32[1,8192]{1,0:T(1,128)} %param.15) | copy-start | bytes 98308
  298.4 4.8 %copy-start.7 = (s32[4]{0:T(128)S(1)}, s32[4]{0:T(128)}, u32[]{:S(2)}) copy-start(s32[4]{0:T(128)} %param.13) | copy-start | bytes 52
  298.4 6.1 %copy-start.3 = (s32[512]{0:T(512)S(1)}, s32[512]{0:T(512)}, u32[]{:S(2)}) copy-start(s32[512]{0:T(512)} %param.12) | copy-start | bytes 6148
  298.4 43.2 %all-to-all-start = ((bf16[16,2,32,768]{3,2,1,0:T(8,128)(2,1)}), bf16[16,2,32,768]{3,2,1,0:T(8,128)(2,1)S(1)}, u32[]{:S(2)}, u32[]{:S(2)}) async-start(bf16[16,2,32,768]{3,2,1,0:T(8,128)(2,1)} %bitcast.170), calls=%async_computation | async-start | bytes 3145728 | tf_op jit(solution)/shard_map/all_to_all | solution.py:66
  304.4 5.7 %copy-start.4 = (s32[512]{0:T(512)S(1)}, s32[512]{0:T(512)}, u32[]{:S(2)}) copy-start(s32[512]{0:T(512)} %param.11) | copy-start | bytes 6148
  346.7 1.4 copy-start.5
  358.4 3.5 copy-start.2
  367.3 3.5 copy-start.2
  376.2 3.5 copy-start.2
  381.3 1.1 copy-start.8
  383.2 13.1 %all-to-all-start.1 = ((f32[16,4,8]{2,1,0:T(4,128)}), f32[16,4,8]{2,1,0:T(4,128)S(1)}, u32[]{:S(2)}, u32[]{:S(2)}) async-start(f32[16,4,8]{2,1,0:T(4,128)} %broadcast_in_dim.50), calls=%async_computation.1 | async-start | bytes 65536 | tf_op jit(solution)/shard_map/all_to_all | solution.py:18
  389.8 7.2 %copy-start.1 = (bf16[1,32,32,1024]{3,2,1,0:T(8,128)(2,1)S(1)}, bf16[1,32,32,1024]{3,2,1,0:T(8,128)(2,1)}, u32[]{:S(2)}) copy-start(bf16[1,32,32,1024]{3,2,1,0:T(8,128)(2,1)} %param.10) | copy-start | bytes 6291460
Sparse Core Ops, SparseCore 0:
  11.6 190.3 all-gather.4
  203.8 74.6 all-gather.6
where the time goes:
time: 404 us
  waiting for transfers between devices  278 us (69%)
  matrix products  43.4 us (11%)
  other arithmetic  34.3 us (8%)
  local copies, waits for them, and re-layouts  22.1 us (5%)
  between operations  14.9 us (4%)
  starting transfers between devices  11.3 us (3%)
    all_gather x1, waiting for transfers between devices, per_device(): local_rows = lax.all_gather(outgoing, 'tensor', axis=2, tiled=True)  190 us
    all_gather x1, waiting for transfers between devices, per_device(): lax.all_gather(qkv_weight[0], 'dp', axis=0, tiled=True)  53.8 us
    all_to_all x1, waiting for transfers between devices, per_device(): lax.all_to_all(outbound, 'dp', split_axis=0, concat_axis=0, tiled=True)  30.5 us
    dot_general x1, matrix products, per_device(): jnp.dot(normed, lax.all_gather(qkv_weight[0], 'dp', axis=0, tiled=True),...  19.8 us
    convert_element_type x1, other arithmetic, per_device(): normed = (as_float * inverse_rms * norm_gain[0]).astype(jnp.bfloat16)  15.4 us
    dot_general x3, matrix products, visit(): jnp.einsum('lsikgh,lckh->lsikgc', queries, block_keys, preferred_element_...  10.8 us
    dot_general x3, matrix products, visit(): jnp.einsum('lsikgc,lckh->lsikgh', block_weights.astype(jnp.bfloat16), blo...  10.4 us
  transfers between devices with their start and end apart: 4, of which 4 were waited for; matrix products, arithmetic and copies ran while one was open for 8% of the time, Pallas kernels for 0%

commit v1 on v0

v1 whole, which is shorter than its diff:
```python
import functools

import jax
import jax.numpy as jnp
from jax import lax
from jax.experimental import pallas as pl
from jax.experimental.pallas import tpu as pltpu
from jax.sharding import PartitionSpec as P


KVH = 8
HD = 128
HQ = 32
GROUP = HQ // KVH

prior_weight = 0.5
norm_eps = 1e-05
LOG2E = 1.4426950408889634


def sent_to_all(value, axis):
    length = lax.axis_size(axis)
    return lax.all_to_all(
        jnp.broadcast_to(value[None], (length, *value.shape)), axis, 0, 0, tiled=True
    )


def y_shift(value, hop):
    pairs = [(y * 2 + h, ((y + hop) % 4) * 2 + h) for y in range(4) for h in range(2)]
    return lax.ppermute(value, "tensor", pairs)


def x_swap(value):
    return lax.ppermute(value, "tensor", [(t, t ^ 1) for t in range(8)])


def z_shift(value, hop):
    pairs = [(z * 2 + c, ((z + hop) % 8) * 2 + c) for z in range(8) for c in range(2)]
    return lax.ppermute(value, "dp", pairs)


def core_swap(value):
    return lax.ppermute(value, "dp", [(d, d ^ 1) for d in range(16)])


def ring_weights(shard):
    half = shard.shape[0] // 2
    up, down = shard, shard
    found = [((0, 0), 0, shard)]
    for step in range(1, 4):
        up, down = z_shift(up, 1), z_shift(down, -1)
        found += [((8 - step, step), 0, up), ((step, step), 0, down)]
    found += [
        ((4, 4), 0, z_shift(up[:half], 1)),
        ((4, 4), half, z_shift(down[half:], -1)),
    ]
    shards = []
    for (hop, step), first, value in found:
        shards.append(((hop, 0, first), value))
        shards.append(((hop, 1, first), core_swap(value)))
    return shards


def mm_kernel(tp_ref, place_ref, sums_ref, gain_ref, *rest, halves, shards, has_acc, last, width):
    count = len(halves)
    copies = sum(2 if h else 1 for h in halves)
    weights, rest = rest[: len(shards)], rest[len(shards) :]
    pieces, rest = rest[:copies], rest[copies:]
    if has_acc:
        acc_in, rest = rest[0], rest[1:]
    out_ref, xbuf, wbuf, acc, xsem, wsem, asem = rest
    rows = xbuf.shape[1]
    half = rows // 2
    position = 0
    for p, is_half in enumerate(halves):
        if is_half:
            for k in range(2):
                pltpu.make_async_copy(
                    pieces[position + k], xbuf.at[p, pl.ds(k * half, half)], xsem.at[p]
                ).start()
            position += 2
        else:
            pltpu.make_async_copy(pieces[position], xbuf.at[p], xsem.at[p]).start()
            position += 1
    for ref, (hop, other, first) in zip(weights, shards):
        block = place_ref[hop]
        start = place_ref[8 + other] + first

        def fetch(ref=ref, block=block, start=start):
            pltpu.make_async_copy(
                ref,
                wbuf.at[block, pl.ds(pl.multiple_of(start, 256), ref.shape[0])],
                wsem.at[block],
            ).start()

        if count == 8:
            fetch()
        else:
            wanted = tp_ref[0] == block
            for p in range(1, count):
                wanted = wanted | (tp_ref[p] == block)
            pl.when(wanted)(fetch)
    if has_acc:
        load = pltpu.make_async_copy(acc_in, acc, asem)
        load.start()
    total = jnp.sum(jnp.transpose(sums_ref[...]), axis=1, keepdims=True)
    inverse = lax.rsqrt(total * (1.0 / width) + norm_eps)
    if has_acc:
        load.wait()
    else:
        acc[...] = jnp.zeros_like(acc)

    def visit(p, carry):
        block = tp_ref[p]
        pltpu.make_async_copy(xbuf.at[p], xbuf.at[p], xsem.at[p]).wait()
        pltpu.make_async_copy(wbuf.at[block], wbuf.at[block], wsem.at[block]).wait()
        gain = gain_ref[pl.ds(block, 1), :]
        normed = (xbuf[p].astype(jnp.float32) * inverse * gain).astype(jnp.bfloat16)
        acc[...] += jnp.dot(normed, wbuf[block], preferred_element_type=jnp.float32)
        return carry

    lax.fori_loop(0, count, visit, 0)
    if last:
        out_ref[...] = acc[...].astype(out_ref.dtype)
    else:
        out_ref[...] = acc[...]


def project(tp, place, sums, gain, weights, pieces, acc=None, last=True):
    shards = tuple(key for key, _ in weights)
    weights = [value for _, value in weights]
    blocks, feats = gain.shape
    columns = weights[0].shape[1]
    rows = sums.shape[1]
    halves = tuple(isinstance(piece, tuple) for piece in pieces)
    flat = []
    for piece in pieces:
        flat.extend(piece if isinstance(piece, tuple) else (piece,))
    count = len(pieces)
    smem = pl.BlockSpec(memory_space=pltpu.SMEM)
    vmem = pl.BlockSpec(memory_space=pltpu.VMEM)
    anyspace = pl.BlockSpec(memory_space=pl.ANY)
    extra = [] if acc is None else [acc]
    return pl.pallas_call(
        functools.partial(
            mm_kernel,
            halves=halves,
            shards=shards,
            has_acc=acc is not None,
            last=last,
            width=feats * blocks,
        ),
        out_shape=jax.ShapeDtypeStruct((rows, columns), jnp.bfloat16 if last else jnp.float32),
        in_specs=[smem, smem, vmem, vmem]
        + [anyspace] * (len(weights) + len(flat) + len(extra)),
        out_specs=vmem,
        scratch_shapes=[
            pltpu.VMEM((count, rows, feats), jnp.bfloat16),
            pltpu.VMEM((blocks, feats, columns), jnp.bfloat16),
            pltpu.VMEM((rows, columns), jnp.float32),
            pltpu.SemaphoreType.DMA((count,)),
            pltpu.SemaphoreType.DMA((blocks,)),
            pltpu.SemaphoreType.DMA,
        ],
        compiler_params=pltpu.CompilerParams(vmem_limit_bytes=44 << 20),
        cost_estimate=pl.CostEstimate(
            flops=2 * rows * columns * feats * count,
            bytes_accessed=2 * count * feats * (rows + columns),
            transcendentals=0,
        ),
        name="project",
    )(tp, place, sums, gain, *weights, *flat, *extra)


def attend_kernel(meta_ref, clen_ref, rows_hbm, cache_ref, score_ref, *rest, seq, has_in):
    if has_in:
        rest = rest[1:]
    ctx_ref, value_ref, rows_ref, obuf, rsems, sems = rest
    steps = rows_ref.shape[0]
    positions = cache_ref.shape[1]
    wide = GROUP * seq
    factor = (HD ** (-0.5)) * LOG2E
    token = lax.broadcasted_iota(jnp.int32, (wide, 1), 0) % seq
    column = lax.broadcasted_iota(jnp.int32, (1, positions), 1)
    causal = lax.broadcasted_iota(jnp.int32, (wide, seq), 1) <= (
        lax.broadcasted_iota(jnp.int32, (wide, seq), 0) % seq
    )
    value_ref[...] = jnp.zeros_like(value_ref)
    weights = jnp.concatenate(
        [jnp.broadcast_to(score_ref[g : g + 1, :], (seq, HD)) for g in range(GROUP)], axis=0
    )
    contract = (((1,), (1,)), ((), ()))

    together = 4

    def load(group):
        part = pl.ds(group * together, together)
        return pltpu.make_async_copy(rows_hbm.at[part], rows_ref.at[part], rsems.at[group])

    for group in range(steps // together):
        load(group).start()

    def visit(group, carry):
        load(group).wait()
        at = [group * together + k for k in range(together)]
        leaf = [meta_ref[0, i] for i in at]
        slot = [meta_ref[1, i] for i in at]
        length = [meta_ref[2, i] for i in at]
        far, own = [], []
        for i, one in zip(at, leaf):
            queries = jnp.concatenate(
                [rows_ref[i, :, g * HD : (g + 1) * HD] for g in range(GROUP)], axis=0
            )
            key_own = rows_ref[i, :, GROUP * HD : (GROUP + 1) * HD]
            far.append(
                lax.dot_general(
                    queries, cache_ref[one, :, :HD], contract, preferred_element_type=jnp.float32
                )
            )
            own.append(
                lax.dot_general(queries, key_own, contract, preferred_element_type=jnp.float32)
            )
        far = [
            f + jnp.where(column < clen_ref[one], 0.0, -jnp.inf) for f, one in zip(far, leaf)
        ]
        own = [jnp.where(causal, o, -jnp.inf) for o in own]
        top = [
            jnp.maximum(jnp.max(f, axis=1, keepdims=True), jnp.max(o, axis=1, keepdims=True))
            for f, o in zip(far, own)
        ]
        far = [jnp.exp2((f - t) * factor) for f, t in zip(far, top)]
        own = [jnp.exp2((o - t) * factor) for o, t in zip(own, top)]
        total = [
            jnp.sum(f, axis=1, keepdims=True) + jnp.sum(o, axis=1, keepdims=True)
            for f, o in zip(far, own)
        ]
        context = [
            jnp.dot(
                f.astype(jnp.bfloat16), cache_ref[one, :, HD:], preferred_element_type=jnp.float32
            )
            + jnp.dot(
                o.astype(jnp.bfloat16),
                rows_ref[i, :, (GROUP + 1) * HD :],
                preferred_element_type=jnp.float32,
            )
            for f, o, one, i in zip(far, own, leaf, at)
        ]
        for c, t, i, place, count in zip(context, total, at, slot, length):
            c = jnp.where(token < count, c * (1.0 / t), 0.0)
            for g in range(GROUP):
                obuf[i, :, g * HD : (g + 1) * HD] = c[g * seq : (g + 1) * seq].astype(
                    jnp.bfloat16
                )
            pltpu.make_async_copy(obuf.at[i], ctx_ref.at[place], sems.at[i]).start()
            scored = jnp.where(token == count - 1, c * weights, 0.0)
            scored = jnp.sum(jnp.sum(scored, axis=0, keepdims=True), axis=1, keepdims=True)
            value_ref[pl.ds(place, 1), :] = jnp.broadcast_to(scored, (1, value_ref.shape[1]))
        return carry

    lax.fori_loop(0, steps // together, visit, 0)
    for i in range(steps):
        pltpu.make_async_copy(obuf.at[i], ctx_ref.at[meta_ref[1, i]], sems.at[i]).wait()


def attend(meta, cache_len, rows, cache, score, slots, earlier=None):
    steps, seq, _ = rows.shape
    smem = pl.BlockSpec(memory_space=pltpu.SMEM)
    vmem = pl.BlockSpec(memory_space=pltpu.VMEM)
    anyspace = pl.BlockSpec(memory_space=pl.ANY)
    extra = [] if earlier is None else [earlier]
    return pl.pallas_call(
        functools.partial(attend_kernel, seq=seq, has_in=earlier is not None),
        out_shape=(
            jax.ShapeDtypeStruct((slots, seq, GROUP * HD), jnp.bfloat16),
            jax.ShapeDtypeStruct((slots, HD), jnp.float32),
        ),
        in_specs=[smem, smem, anyspace, vmem, vmem] + [anyspace] * len(extra),
        out_specs=(anyspace, vmem),
        scratch_shapes=[
            pltpu.VMEM(rows.shape, jnp.bfloat16),
            pltpu.VMEM((steps, seq, GROUP * HD), jnp.bfloat16),
            pltpu.SemaphoreType.DMA((steps // 4,)),
            pltpu.SemaphoreType.DMA((steps,)),
        ],
        input_output_aliases={} if earlier is None else {5: 0},
        compiler_params=pltpu.CompilerParams(vmem_limit_bytes=24 << 20),
        cost_estimate=pl.CostEstimate(
            flops=4 * steps * GROUP * seq * cache.shape[1] * HD,
            bytes_accessed=2 * (rows.size + cache.size + slots * seq * GROUP * HD),
            transcendentals=steps * GROUP * seq * cache.shape[1],
        ),
        name="attend",
    )(meta, cache_len, rows, cache, score, *extra)


def staged(
    step_embeds, step_len, leaf_of_step, cache_len, caches, norm_gain, qkv_weight, score_weight
):
    embeds = step_embeds[0]
    steps_here, seq, feats = embeds.shape
    leaves_here = cache_len.shape[0]
    per_leaf = steps_here // leaves_here
    peers = lax.axis_size("dp")
    me = lax.axis_index("dp")
    tensor = lax.axis_index("tensor")
    rows = peers * seq

    weights = ring_weights(qkv_weight[0])
    z, core = me // 2, me % 2
    place = jnp.concatenate(
        [
            (z + jnp.arange(8, dtype=jnp.int32)) % 8,
            jnp.stack([core, 1 - core]) * qkv_weight.shape[1],
        ]
    ).astype(jnp.int32)

    leaves = leaf_of_step.reshape(peers, steps_here)
    lengths = step_len.reshape(peers, steps_here)
    index = jnp.arange(steps_here, dtype=jnp.int32)
    earlier = index[None, :] < index[:, None]
    mine = lax.dynamic_index_in_dim(leaves, me, 0, keepdims=False) // leaves_here
    same = mine[None, :] == mine[:, None]
    turn = jnp.sum(same & earlier, axis=1)
    to_peer = mine[None, :] == jnp.arange(peers, dtype=jnp.int32)[:, None]
    send = [
        jnp.sum(jnp.where(to_peer & (turn == s)[None, :], index[None, :], 0), axis=1)
        for s in range(2)
    ]
    early_rows = embeds[send[0]].reshape(rows, feats)
    late_rows = embeds[send[1]]
    late_rows = lax.all_to_all(late_rows, "dp", 0, 0, tiled=True).reshape(rows, feats)

    here = (leaves // leaves_here) == me
    ordinal = jnp.sum(here[:, None, :] & earlier[None], axis=2)
    marks = jnp.stack([here & (ordinal == s) for s in range(2)])
    ids = index[None, :] + steps_here * jnp.arange(peers, dtype=jnp.int32)[:, None]
    arrive_id = jnp.sum(jnp.where(marks, ids[None], 0), axis=2).reshape(-1)
    arrive_leaf = jnp.sum(jnp.where(marks, leaves[None], 0), axis=2).reshape(-1)
    arrive_leaf = arrive_leaf - me * leaves_here
    arrive_len = jnp.sum(jnp.where(marks, lengths[None], 0), axis=2).reshape(-1)
    rank = jnp.sum(
        (arrive_leaf[None, :] == arrive_leaf[:, None])
        & (arrive_id[None, :] < arrive_id[:, None]),
        axis=1,
    )
    slot = jnp.clip(arrive_leaf * per_leaf + rank, 0, steps_here - 1)
    arrive_leaf = jnp.clip(arrive_leaf, 0, leaves_here - 1)
    meta = jnp.stack([arrive_leaf, slot, arrive_len]).astype(jnp.int32)

    a, b = early_rows, late_rows
    a_x = x_swap(a)
    a_left, a_right = y_shift(a, 1), y_shift(a, -1)
    b_left, b_right = y_shift(b, 1), y_shift(b, -1)
    b_x = x_swap(b)
    ax_left = y_shift(a_x, 1)
    ax_right = y_shift(a_x, -1)
    a_far = y_shift(a_left, 1)
    ax_far = y_shift(ax_right, -1)
    bx_left = x_swap(b_left)
    bx_right = x_swap(b_right)
    b_far = y_shift(b_right, -1)
    bx_far = y_shift(bx_left, 1)

    squares = [
        jnp.sum(jnp.square(part.astype(jnp.float32)), axis=1) for part in (a, b)
    ]
    sums = sent_to_all(jnp.concatenate(squares), "tensor")
    sums_a, sums_b = sums[:, :rows], sums[:, rows:]

    y, h = tensor // 2, tensor % 2

    def owner(dy, dx):
        return ((y + dy) % 4) * 2 + ((h + dx) % 2)

    first = [owner(0, 0), owner(-1, 0), owner(1, 0), owner(0, 1), owner(-1, 1)]
    then = [owner(1, 1), owner(2, 0), owner(2, 1)]
    gain = norm_gain[0].reshape(-1, feats)
    out_a = project(
      jnp.stack(first + then).astype(jnp.int32),
      place,
      sums_a,
      gain,
      weights,
      [a, a_left, a_right, a_x, ax_left, ax_right, a_far, ax_far],
    )
    part_b = project(
      jnp.stack(first).astype(jnp.int32),
      place,
      sums_b,
      gain,
      weights,
      [b, b_left, b_right, b_x, bx_left],
      last=False,
    )
    out_b = project(
        jnp.stack(then).astype(jnp.int32), place, sums_b, gain, weights, [bx_right, b_far, bx_far], acc=part_b
    )

    out_a = lax.all_to_all(out_a.reshape(peers, seq, -1), "dp", 0, 0, tiled=True)
    out_b = out_b.reshape(peers, seq, -1)
    cache = caches[0]
    score = score_weight[0].reshape(GROUP, HD)
    context, value_b = attend(meta[:, peers:], cache_len, out_b, cache, score, steps_here)
    context, value_a = attend(
        meta[:, :peers], cache_len, out_a, cache, score, steps_here, earlier=context
    )
    contexts = context.reshape(1, leaves_here, per_leaf, seq, GROUP * HD)
    model_weight = jnp.where(lax.axis_index("mp") == 0, prior_weight, 1.0).astype(jnp.float32)
    partial = (value_a + value_b)[:, 0].reshape(leaves_here, per_leaf) * model_weight
    step_value = jnp.sum(sent_to_all(partial, ("tensor", "mp")), axis=0)
    return (contexts, step_value)


def solution(mesh):
    placed = (
        P("mp", "dp", None, "tensor"),
        P(),
        P(),
        P("dp"),
        P("mp", "dp", None, "tensor"),
        P("mp", None),
        P("mp", "dp", "tensor"),
        P("mp", "tensor"),
    )
    return jax.shard_map(
        staged,
        mesh=mesh,
        in_specs=placed,
        out_specs=(P("mp", "dp", None, None, "tensor"), P("dp", None)),
        check_vma=False,
    )
```

time: 404 us -> 270 us (0.67); the launches traced: 404 us -> 265 us
  waiting for transfers between devices: 278 us -> 112 us
  starting transfers between devices: 11.3 us -> 76.1 us
  matrix products: 43.4 us -> 0 us
  Pallas kernels: 0 us -> 42.2 us
  other arithmetic: 34.3 us -> 4.65 us
  between operations: 14.9 us -> 1.07 us
  blocking collectives: 0 us -> 8.99 us
    all_gather x2 -> x0, waiting for transfers between devices: 244 us -> none  [the longest x1 190 us: per_device(): local_rows = lax.all_gather(outgoing, 'tensor', axis=2, tiled=True)]
    ppermute x0 -> x31, waiting for transfers between devices: none -> 107 us  [the longest x10 47.5 us: y_shift(): return lax.ppermute(value, 'tensor', pairs)]
    ppermute x0 -> x31, starting transfers between devices: none -> 54.2 us  [the longest x9 20.5 us: core_swap(): return lax.ppermute(value, 'dp', [(d, d ^ 1) for d in range(16)])]
    dot_general x9 -> x0, matrix products: 43.4 us -> none  [the longest x1 19.8 us: per_device(): jnp.dot(normed, lax.all_gather(qkv_weight[0], 'dp', axis=0, tiled=True),...]
    pallas_call x0 -> x5, Pallas kernels: none -> 42.2 us  [the longest x3 29.5 us: project(): pl.pallas_call(functools.partial(mm_kernel, halves=halves, shards=shards,...]
    all_to_all x1 -> x2, waiting for transfers between devices: 30.5 us -> 0.01 us  [the longest x1 0.01 us: staged(): lax.all_to_all(out_a.reshape(peers, seq, -1), 'dp', 0, 0, tiled=True)]
    convert_element_type x2 -> x0, other arithmetic: 15.5 us -> none  [the longest x1 15.4 us: per_device(): normed = (as_float * inverse_rms * norm_gain[0]).astype(jnp.bfloat16)]
    all_to_all x1 -> x2, starting transfers between devices: 4.67 us -> 17.9 us  [the longest x1 11.1 us: staged(): lax.all_to_all(out_a.reshape(peers, seq, -1), 'dp', 0, 0, tiled=True)]
  transfers between devices with their start and end apart: 4 -> 34, of which waited for: 4 -> 13; matrix products, arithmetic and copies ran while one was open for 8% -> 4% of each run, Pallas kernels for 0% -> 14%
where the time goes in v1:
time: 270 us; the launch traced here: 265 us
  waiting for transfers between devices  112 us (41%)
  starting transfers between devices  76.1 us (28%)
  Pallas kernels  42.2 us (16%)
  local copies, waits for them, and re-layouts  20.1 us (7%)
  blocking collectives  8.99 us (3%)
  other arithmetic  4.65 us (2%)
    ppermute x10, waiting for transfers between devices, y_shift(): return lax.ppermute(value, 'tensor', pairs)  47.5 us
    ppermute x8, waiting for transfers between devices, z_shift(): return lax.ppermute(value, 'dp', pairs)  35.6 us
    pallas_call x3, Pallas kernels, project(): pl.pallas_call(functools.partial(mm_kernel, halves=halves, shards=shards,...  29.5 us
    ppermute x4, waiting for transfers between devices, x_swap(): return lax.ppermute(value, 'tensor', [(t, t ^ 1) for t in range(8)])  23.9 us
    ppermute x9, starting transfers between devices, core_swap(): return lax.ppermute(value, 'dp', [(d, d ^ 1) for d in range(16)])  20.5 us
    ppermute x10, starting transfers between devices, y_shift(): return lax.ppermute(value, 'tensor', pairs)  14.4 us
    ppermute x8, starting transfers between devices, z_shift(): return lax.ppermute(value, 'dp', pairs)  13 us
    pallas_call x2, Pallas kernels, attend(): pl.pallas_call(functools.partial(attend_kernel, seq=seq, has_in=earlier i...  12.7 us
  transfers between devices with their start and end apart: 34, of which 13 were waited for; matrix products, arithmetic and copies ran while one was open for 4% of the time, Pallas kernels for 14%

profile of v1, /device:TPU:1, one launch (start us, length us, event | category | flops | bytes accessed | tf_op | source)
XLA Modules:
  0.0 265.2 jit_solution(15780171647174277830)
XLA Ops:
  0.6 6.5 %collective-permute-start.3 = (bf16[512,768]{1,0:T(8,128)(2,1)}, bf16[512,768]{1,0:T(8,128)(2,1)S(1)}, u32[]{:S(2)}, u32[]{:S(2)}) collective-permute-start(bf16[512,768]{1,0:T(8,128)(2,1)} %bitcast.50), channel_id=1, source_target_pairs={{0,224},{16,240},{32,0},{48,16},{64,32},{80,48},{96,64},{112,80},{... | collective-permute-start | bytes 2359304 | tf_op jit(solution)/shard_map/ppermute | solution.py:39
  16.3 7.4 %collective-permute-done.3.rest_4_ = bf16[512,768]{1,0:T(8,128)(2,1)S(1)} collective-permute-done((bf16[512,768]{1,0:T(8,128)(2,1)}, bf16[512,768]{1,0:T(8,128)(2,1)S(1)}, u32[]{:S(2)}, u32[]{:S(2)}) %collective-permute-start.3) | collective-permute-done | bytes 786464 | tf_op jit(solution)/shard_map/ppermute | solution.py:39
  26.6 6.8 %all-to-all-start = ((bf16[16,32,1024]{2,1,0:T(8,128)(2,1)}), bf16[16,32,1024]{2,1,0:T(8,128)(2,1)}, u32[]{:S(2)}, u32[]{:S(2)}) async-start(bf16[16,32,1024]{2,1,0:T(8,128)(2,1)} %gather_fusion.1), calls=%async_computation | async-start | bytes 2097152 | tf_op jit(solution)/shard_map/all_to_all | solution.py:331
  38.8 3.4 %collective-permute-start.21 = (bf16[512,1024]{1,0:T(8,128)(2,1)}, bf16[512,1024]{1,0:T(8,128)(2,1)}, u32[]{:S(2)}, u32[]{:S(2)}) collective-permute-start(bf16[512,1024]{1,0:T(8,128)(2,1)} %collective-permute-done.19.rest_21_), channel_id=1, source_target_pairs={{0,12},{2,14},{4,0},{6,2},{8,4},{10,6},{12,8},{14,10},{1,13},{3,15... | collective-permute-start | bytes 3145736 | tf_op jit(solution)/shard_map/ppermute | solution.py:30
  42.3 6.2 %collective-permute-done.17.rest_19_ = bf16[512,1024]{1,0:T(8,128)(2,1)} collective-permute-done((bf16[512,1024]{1,0:T(8,128)(2,1)}, bf16[512,1024]{1,0:T(8,128)(2,1)}, u32[]{:S(2)}, u32[]{:S(2)}) %collective-permute-start.17) | collective-permute-done | bytes 1048608 | tf_op jit(solution)/shard_map/ppermute | solution.py:30
  50.8 24.2 %collective-permute-done.7.rest_8_ = bf16[512,768]{1,0:T(8,128)(2,1)} collective-permute-done((bf16[512,768]{1,0:T(8,128)(2,1)S(1)}, bf16[512,768]{1,0:T(8,128)(2,1)}, u32[]{:S(2)}, u32[]{:S(2)}) %collective-permute-start.7) | collective-permute-done | bytes 786464 | tf_op jit(solution)/shard_map/ppermute | solution.py:39
  82.5 17.8 %collective-permute-done.20.rest_22_ = bf16[512,1024]{1,0:T(8,128)(2,1)} collective-permute-done((bf16[512,1024]{1,0:T(8,128)(2,1)}, bf16[512,1024]{1,0:T(8,128)(2,1)}, u32[]{:S(2)}, u32[]{:S(2)}) %collective-permute-start.20) | collective-permute-done | bytes 1048608 | tf_op jit(solution)/shard_map/ppermute | solution.py:30
  100.3 3.3 %collective-permute-start.6 = (bf16[512,768]{1,0:T(8,128)(2,1)}, bf16[512,768]{1,0:T(8,128)(2,1)}, u32[]{:S(2)}, u32[]{:S(2)}) collective-permute-start(bf16[512,768]{1,0:T(8,128)(2,1)} %collective-permute-done.5.rest_6_), channel_id=1, source_target_pairs={{0,16},{16,0},{32,48},{48,32},{64,80},{80,64},{96,112},{112,96},{1... | collective-permute-start | bytes 2359304 | tf_op jit(solution)/shard_map/ppermute | solution.py:43
  103.7 19.1 %collective-permute-done.22.rest_24_ = bf16[512,1024]{1,0:T(8,128)(2,1)} collective-permute-done((bf16[512,1024]{1,0:T(8,128)(2,1)}, bf16[512,1024]{1,0:T(8,128)(2,1)}, u32[]{:S(2)}, u32[]{:S(2)}) %collective-permute-start.22) | collective-permute-done | bytes 1048608 | tf_op jit(solution)/shard_map/ppermute | solution.py:30
  132.6 2.9 %collective-permute-done.15.rest_16_ = bf16[256,768]{1,0:T(8,128)(2,1)S(1)} collective-permute-done((bf16[256,768]{1,0:T(8,128)(2,1)S(1)}, bf16[256,768]{1,0:T(8,128)(2,1)S(1)}, u32[]{:S(2)}, u32[]{:S(2)}) %collective-permute-start.15) | collective-permute-done | bytes 393248 | tf_op jit(solution)/shard_map/ppermute | solution.py:39
  135.5 3.0 %collective-permute-start.10 = (bf16[512,768]{1,0:T(8,128)(2,1)S(1)}, bf16[512,768]{1,0:T(8,128)(2,1)}, u32[]{:S(2)}, u32[]{:S(2)}) collective-permute-start(bf16[512,768]{1,0:T(8,128)(2,1)S(1)} %collective-permute-done.9.rest_10_), channel_id=1, source_target_pairs={{0,16},{16,0},{32,48},{48,32},{64,80},{80,64},{96,112},{112,96},{1... | collective-permute-start | bytes 2359304 | tf_op jit(solution)/shard_map/ppermute | solution.py:43
  139.7 3.1 %collective-permute-start.16 = (bf16[256,768]{1,0:T(8,128)(2,1)S(1)}, bf16[256,768]{1,0:T(8,128)(2,1)}, u32[]{:S(2)}, u32[]{:S(2)}) collective-permute-start(bf16[256,768]{1,0:T(8,128)(2,1)S(1)} %collective-permute-done.15.rest_16_), channel_id=1, source_target_pairs={{0,16},{16,0},{32,48},{48,32},{64,80},{80,64},{96,112},{112,96},{1... | collective-permute-start | bytes 1179656 | tf_op jit(solution)/shard_map/ppermute | solution.py:43
  144.4 2.8 %collective-permute-done.27.rest_19_ = bf16[512,1024]{1,0:T(8,128)(2,1)} collective-permute-done((bf16[512,1024]{1,0:T(8,128)(2,1)}, bf16[512,1024]{1,0:T(8,128)(2,1)}, u32[]{:S(2)}, u32[]{:S(2)}) %collective-permute-start.27) | collective-permute-done | bytes 1048608 | tf_op jit(solution)/shard_map/ppermute | solution.py:30
  150.5 4.0 %all-to-all-start.1 = ((f32[8,1,1024]{2,1,0:T(1,128)}), f32[8,1,1024]{2,1,0:T(1,128)S(1)}, u32[]{:S(2)}, u32[]{:S(2)}) async-start(f32[8,1,1024]{2,1,0:T(1,128)} %broadcast_in_dim.74), calls=%async_computation.1 | async-start | bytes 65536 | tf_op jit(solution)/shard_map/all_to_all | solution.py:23
  156.1 5.1 %all-to-all-done.1 = f32[8,1,1024]{2,1,0:T(1,128)S(1)} async-done(((f32[8,1,1024]{2,1,0:T(1,128)}), f32[8,1,1024]{2,1,0:T(1,128)S(1)}, u32[]{:S(2)}, u32[]{:S(2)}) %all-to-all-start.1) | async-done | bytes 32800 | tf_op jit(solution)/shard_map/all_to_all | solution.py:23
  168.6 12.4 %project.3 = bf16[512,768]{1,0:T(8,128)(2,1)S(1)} custom-call(s32[8]{0:T(128)S(1)} %stack.70.tp_ref, s32[10]{0:T(128)S(1)} %pad_add_fusion.2.place_ref, f32[8,512]{1,0:T(8,128)S(1)} %get-tuple-element.20.sums_ref, f32[8,1024]{1,0:T(8,128)S(1)} %reshape_squeeze.7.gain_ref, bf16[512,768]{1,0:T(8,128)(2,1)S(1)} %bitcast.53, ...), custom_call_target="tpu_custom_call" | custom-call | flops 6442450944 | bytes 20971520 | tf_op jit(solution)/shard_map/project/pallas_call | solution.py:144
  181.8 11.1 %all-to-all-start.2 = ((bf16[16,32,768]{2,1,0:T(8,128)(2,1)}), bf16[16,32,768]{2,1,0:T(8,128)(2,1)}, u32[]{:S(2)}, u32[]{:S(2)}) async-start(bf16[16,32,768]{2,1,0:T(8,128)(2,1)} %bitcast.58), calls=%async_computation.2 | async-start | bytes 1572864 | tf_op jit(solution)/shard_map/all_to_all | solution.py:399
  195.4 14.0 %collective-permute-done.30.rest_21_ = bf16[512,1024]{1,0:T(8,128)(2,1)} collective-permute-done((bf16[512,1024]{1,0:T(8,128)(2,1)}, bf16[512,1024]{1,0:T(8,128)(2,1)}, u32[]{:S(2)}, u32[]{:S(2)}) %collective-permute-start.30) | collective-permute-done | bytes 1048608 | tf_op jit(solution)/shard_map/ppermute | solution.py:34
  212.9 9.7 %project.4.rest_21_ = f32[512,768]{1,0:T(8,128)} custom-call(s32[5]{0:T(128)S(1)} %stack.75.tp_ref, s32[10]{0:T(128)S(1)} %pad_add_fusion.2.place_ref, f32[8,512]{1,0:T(8,128)S(1)} %get-tuple-element.19.sums_ref, f32[8,1024]{1,0:T(8,128)S(1)} %reshape_squeeze.7.gain_ref, bf16[512,768]{1,0:T(8,128)(2,1)S(1)} %bitcast.54, ...), custom_call_target="tpu_custom_call" | custom-call | flops 4026531840 | bytes 13107200 | tf_op jit(solution)/shard_map/project/pallas_call | solution.py:144
  222.6 9.2 %collective-permute-done.25.rest_18_ = bf16[512,1024]{1,0:T(8,128)(2,1)S(1)} collective-permute-done((bf16[512,1024]{1,0:T(8,128)(2,1)}, bf16[512,1024]{1,0:T(8,128)(2,1)S(1)}, u32[]{:S(2)}, u32[]{:S(2)}) %collective-permute-start.25) | collective-permute-done | bytes 1048608 | tf_op jit(solution)/shard_map/ppermute | solution.py:34
  233.8 7.4 %project.5 = bf16[512,768]{1,0:T(8,128)(2,1)S(1)} custom-call(s32[3]{0:T(128)S(1)} %pad_add_fusion.3.tp_ref, s32[10]{0:T(128)S(1)} %pad_add_fusion.2.place_ref, f32[8,512]{1,0:T(8,128)S(1)} %get-tuple-element.19.sums_ref, f32[8,1024]{1,0:T(8,128)S(1)} %reshape_squeeze.7.gain_ref, bf16[512,768]{1,0:T(8,128)(2,1)S(1)} %bitcast.55, ...), custom_call_target="tpu_custom_call" | custom-call | flops 2415919104 | bytes 7864320 | tf_op jit(solution)/shard_map/project/pallas_call | solution.py:144
  241.3 6.4 %attend.2 = (bf16[32,32,512]{2,1,0:T(8,128)(2,1)}, f32[32,128]{1,0:T(8,128)S(1)}) custom-call(s32[3,16]{1,0:T(4,128)S(1)} %get-tuple-element.21.meta_ref, s32[4]{0:T(128)S(1)} %copy-done.15, bf16[16,32,768]{2,1,0:T(8,128)(2,1)S(1)} %bitcast.59, bf16[4,768,256]{2,1,0:T(8,128)(2,1)S(1)} %bitcast.56, f32[4,128]{1,0:T(4,128)S(1)} %bitcast.60), custom_call_target="tpu_custom_call" | custom-call | flops 805306368 | bytes 3407872 | tf_op jit(solution)/shard_map/attend/pallas_call | solution.py:271
  249.1 6.3 %attend.3 = (bf16[32,32,512]{2,1,0:T(8,128)(2,1)}, f32[32,128]{1,0:T(8,128)S(1)}) custom-call(s32[3,16]{1,0:T(4,128)S(1)} %get-tuple-element.22.meta_ref, s32[4]{0:T(128)S(1)} %copy-done.15, bf16[16,32,768]{2,1,0:T(8,128)(2,1)} %all-to-all-done.2.rows_hbm, bf16[4,768,256]{2,1,0:T(8,128)(2,1)S(1)} %bitcast.57, ...), custom_call_target="tpu_custom_call", output_to_operand_aliasing={{0}: (5, {})} | custom-call | flops 805306368 | bytes 3407872 | tf_op jit(solution)/shard_map/attend/pallas_call | solution.py:271
  255.6 9.0 %all_to_all.24 = f32[16,4,8]{2,1,0:T(4,128)S(1)} all-to-all(f32[16,4,8]{2,1,0:T(4,128)S(1)} %broadcast_in_dim.75), channel_id=1, replica_groups=mesh['dp'=16,'tensor'=8,'mp'=2] {'tensor','mp'}, dimensions={0} | all-to-all | bytes 4096 | tf_op jit(solution)/shard_map/all_to_all | solution.py:23
  (151 shorter events, 62.9 us)
Async XLA Ops:
  7.1 26.2 %collective-permute-start.1 = (bf16[512,768]{1,0:T(8,128)(2,1)}, bf16[512,768]{1,0:T(8,128)(2,1)}, u32[]{:S(2)}, u32[]{:S(2)}) collective-permute-start(bf16[512,768]{1,0:T(8,128)(2,1)} %bitcast.51), channel_id=1, source_target_pairs={{0,32},{16,48},{32,64},{48,80},{64,96},{80,112},{96,128},{112,144}... | collective-permute-start | bytes 2359304 | tf_op jit(solution)/shard_map/ppermute | solution.py:39
  7.1 28.9 %collective-permute-start = (bf16[512,768]{1,0:T(8,128)(2,1)}, bf16[512,768]{1,0:T(8,128)(2,1)}, u32[]{:S(2)}, u32[]{:S(2)}) collective-permute-start(bf16[512,768]{1,0:T(8,128)(2,1)} %bitcast.52), channel_id=1, source_target_pairs={{0,16},{16,0},{32,48},{48,32},{64,80},{80,64},{96,112},{112,96},{1... | collective-permute-start | bytes 2359304 | tf_op jit(solution)/shard_map/ppermute | solution.py:43
  10.8 26.5 %collective-permute-start.19 = (bf16[512,1024]{1,0:T(8,128)(2,1)}, bf16[512,1024]{1,0:T(8,128)(2,1)}, u32[]{:S(2)}, u32[]{:S(2)}) collective-permute-start(bf16[512,1024]{1,0:T(8,128)(2,1)} %bitcast.62), channel_id=1, source_target_pairs={{0,2},{2,0},{4,6},{6,4},{8,10},{10,8},{12,14},{14,12},{1,3},{3,1},... | collective-permute-start | bytes 3145736 | tf_op jit(solution)/shard_map/ppermute | solution.py:34
  26.6 77.1 %all-to-all-start = ((bf16[16,32,1024]{2,1,0:T(8,128)(2,1)}), bf16[16,32,1024]{2,1,0:T(8,128)(2,1)}, u32[]{:S(2)}, u32[]{:S(2)}) async-start(bf16[16,32,1024]{2,1,0:T(8,128)(2,1)} %gather_fusion.1), calls=%async_computation | async-start | bytes 2097152 | tf_op jit(solution)/shard_map/all_to_all | solution.py:331
  33.4 41.7 %collective-permute-start.7 = (bf16[512,768]{1,0:T(8,128)(2,1)S(1)}, bf16[512,768]{1,0:T(8,128)(2,1)}, u32[]{:S(2)}, u32[]{:S(2)}) collective-permute-start(bf16[512,768]{1,0:T(8,128)(2,1)S(1)} %collective-permute-done.3.rest_4_), channel_id=1, source_target_pairs={{0,224},{16,240},{32,0},{48,16},{64,32},{80,48},{96,64},{112,80},{... | collective-permute-start | bytes 2359304 | tf_op jit(solution)/shard_map/ppermute | solution.py:39
  36.0 40.3 %collective-permute-start.4 = (bf16[512,768]{1,0:T(8,128)(2,1)S(1)}, bf16[512,768]{1,0:T(8,128)(2,1)S(1)}, u32[]{:S(2)}, u32[]{:S(2)}) collective-permute-start(bf16[512,768]{1,0:T(8,128)(2,1)S(1)} %collective-permute-done.3.rest_4_), channel_id=1, source_target_pairs={{0,16},{16,0},{32,48},{48,32},{64,80},{80,64},{96,112},{112,96},{1... | collective-permute-start | bytes 2359304 | tf_op jit(solution)/shard_map/ppermute | solution.py:43
  37.4 40.9 %collective-permute-start.5 = (bf16[512,768]{1,0:T(8,128)(2,1)}, bf16[512,768]{1,0:T(8,128)(2,1)}, u32[]{:S(2)}, u32[]{:S(2)}) collective-permute-start(bf16[512,768]{1,0:T(8,128)(2,1)} %collective-permute-done.1.rest_2_), channel_id=1, source_target_pairs={{0,32},{16,48},{32,64},{48,80},{64,96},{80,112},{96,128},{112,144}... | collective-permute-start | bytes 2359304 | tf_op jit(solution)/shard_map/ppermute | solution.py:39
  38.8 41.7 %collective-permute-start.21 = (bf16[512,1024]{1,0:T(8,128)(2,1)}, bf16[512,1024]{1,0:T(8,128)(2,1)}, u32[]{:S(2)}, u32[]{:S(2)}) collective-permute-start(bf16[512,1024]{1,0:T(8,128)(2,1)} %collective-permute-done.19.rest_21_), channel_id=1, source_target_pairs={{0,12},{2,14},{4,0},{6,2},{8,4},{10,6},{12,8},{14,10},{1,13},{3,15... | collective-permute-start | bytes 3145736 | tf_op jit(solution)/shard_map/ppermute | solution.py:30
  48.5 32.0 %collective-permute-start.2 = (bf16[512,768]{1,0:T(8,128)(2,1)}, bf16[512,768]{1,0:T(8,128)(2,1)}, u32[]{:S(2)}, u32[]{:S(2)}) collective-permute-start(bf16[512,768]{1,0:T(8,128)(2,1)} %collective-permute-done.1.rest_2_), channel_id=1, source_target_pairs={{0,16},{16,0},{32,48},{48,32},{64,80},{80,64},{96,112},{112,96},{1... | collective-permute-start | bytes 2359304 | tf_op jit(solution)/shard_map/ppermute | solution.py:43
  77.3 45.5 %collective-permute-start.22 = (bf16[512,1024]{1,0:T(8,128)(2,1)}, bf16[512,1024]{1,0:T(8,128)(2,1)}, u32[]{:S(2)}, u32[]{:S(2)}) collective-permute-start(bf16[512,1024]{1,0:T(8,128)(2,1)} %collective-permute-done.17.rest_19_), channel_id=1, source_target_pairs={{0,4},{2,6},{4,8},{6,10},{8,12},{10,14},{12,0},{14,2},{1,5},{3,7},... | collective-permute-start | bytes 3145736 | tf_op jit(solution)/shard_map/ppermute | solution.py:30
  78.3 44.7 %collective-permute-start.11 = (bf16[512,768]{1,0:T(8,128)(2,1)}, bf16[512,768]{1,0:T(8,128)(2,1)}, u32[]{:S(2)}, u32[]{:S(2)}) collective-permute-start(bf16[512,768]{1,0:T(8,128)(2,1)} %collective-permute-done.7.rest_8_), channel_id=1, source_target_pairs={{0,224},{16,240},{32,0},{48,16},{64,32},{80,48},{96,64},{112,80},{... | collective-permute-start | bytes 2359304 | tf_op jit(solution)/shard_map/ppermute | solution.py:39
  80.5 46.4 %collective-permute-start.9 = (bf16[512,768]{1,0:T(8,128)(2,1)}, bf16[512,768]{1,0:T(8,128)(2,1)S(1)}, u32[]{:S(2)}, u32[]{:S(2)}) collective-permute-start(bf16[512,768]{1,0:T(8,128)(2,1)} %collective-permute-done.5.rest_6_), channel_id=1, source_target_pairs={{0,32},{16,48},{32,64},{48,80},{64,96},{80,112},{96,128},{112,144}... | collective-permute-start | bytes 2359304 | tf_op jit(solution)/shard_map/ppermute | solution.py:39
  80.6 49.3 %collective-permute-start.8 = (bf16[512,768]{1,0:T(8,128)(2,1)}, bf16[512,768]{1,0:T(8,128)(2,1)}, u32[]{:S(2)}, u32[]{:S(2)}) collective-permute-start(bf16[512,768]{1,0:T(8,128)(2,1)} %collective-permute-done.7.rest_8_), channel_id=1, source_target_pairs={{0,16},{16,0},{32,48},{48,32},{64,80},{80,64},{96,112},{112,96},{1... | collective-permute-start | bytes 2359304 | tf_op jit(solution)/shard_map/ppermute | solution.py:43
  100.3 29.8 %collective-permute-start.6 = (bf16[512,768]{1,0:T(8,128)(2,1)}, bf16[512,768]{1,0:T(8,128)(2,1)}, u32[]{:S(2)}, u32[]{:S(2)}) collective-permute-start(bf16[512,768]{1,0:T(8,128)(2,1)} %collective-permute-done.5.rest_6_), channel_id=1, source_target_pairs={{0,16},{16,0},{32,48},{48,32},{64,80},{80,64},{96,112},{112,96},{1... | collective-permute-start | bytes 2359304 | tf_op jit(solution)/shard_map/ppermute | solution.py:43
  123.0 38.2 %collective-permute-start.23 = (bf16[512,1024]{1,0:T(8,128)(2,1)}, bf16[512,1024]{1,0:T(8,128)(2,1)}, u32[]{:S(2)}, u32[]{:S(2)}) collective-permute-start(bf16[512,1024]{1,0:T(8,128)(2,1)} %collective-permute-done.21.rest_23_), channel_id=1, source_target_pairs={{0,12},{2,14},{4,0},{6,2},{8,4},{10,6},{12,8},{14,10},{1,13},{3,15... | collective-permute-start | bytes 3145736 | tf_op jit(solution)/shard_map/ppermute | solution.py:30
  130.1 32.7 %collective-permute-start.12 = (bf16[512,768]{1,0:T(8,128)(2,1)}, bf16[512,768]{1,0:T(8,128)(2,1)}, u32[]{:S(2)}, u32[]{:S(2)}) collective-permute-start(bf16[512,768]{1,0:T(8,128)(2,1)} %collective-permute-done.11.rest_12_), channel_id=1, source_target_pairs={{0,16},{16,0},{32,48},{48,32},{64,80},{80,64},{96,112},{112,96},{1... | collective-permute-start | bytes 2359304 | tf_op jit(solution)/shard_map/ppermute | solution.py:43
  135.5 29.7 %collective-permute-start.10 = (bf16[512,768]{1,0:T(8,128)(2,1)S(1)}, bf16[512,768]{1,0:T(8,128)(2,1)}, u32[]{:S(2)}, u32[]{:S(2)}) collective-permute-start(bf16[512,768]{1,0:T(8,128)(2,1)S(1)} %collective-permute-done.9.rest_10_), channel_id=1, source_target_pairs={{0,16},{16,0},{32,48},{48,32},{64,80},{80,64},{96,112},{112,96},{1... | collective-permute-start | bytes 2359304 | tf_op jit(solution)/shard_map/ppermute | solution.py:43
  161.2 32.4 %collective-permute-start.24 = (bf16[512,1024]{1,0:T(8,128)(2,1)}, bf16[512,1024]{1,0:T(8,128)(2,1)}, u32[]{:S(2)}, u32[]{:S(2)}) collective-permute-start(bf16[512,1024]{1,0:T(8,128)(2,1)} %bitcast.25.rest_18_), channel_id=1, source_target_pairs={{0,12},{2,14},{4,0},{6,2},{8,4},{10,6},{12,8},{14,10},{1,13},{3,15... | collective-permute-start | bytes 3145736 | tf_op jit(solution)/shard_map/ppermute | solution.py:30
  162.2 32.8 %collective-permute-start.28 = (bf16[512,1024]{1,0:T(8,128)(2,1)}, bf16[512,1024]{1,0:T(8,128)(2,1)}, u32[]{:S(2)}, u32[]{:S(2)}) collective-permute-start(bf16[512,1024]{1,0:T(8,128)(2,1)} %collective-permute-done.27.rest_19_), channel_id=1, source_target_pairs={{0,2},{2,0},{4,6},{6,4},{8,10},{10,8},{12,14},{14,12},{1,3},{3,1},... | collective-permute-start | bytes 3145736 | tf_op jit(solution)/shard_map/ppermute | solution.py:34
  162.8 46.6 %collective-permute-start.30 = (bf16[512,1024]{1,0:T(8,128)(2,1)}, bf16[512,1024]{1,0:T(8,128)(2,1)}, u32[]{:S(2)}, u32[]{:S(2)}) collective-permute-start(bf16[512,1024]{1,0:T(8,128)(2,1)} %bitcast.25.rest_18_), channel_id=1, source_target_pairs={{0,2},{2,0},{4,6},{6,4},{8,10},{10,8},{12,14},{14,12},{1,3},{3,1},... | collective-permute-start | bytes 3145736 | tf_op jit(solution)/shard_map/ppermute | solution.py:34
  181.8 65.9 %all-to-all-start.2 = ((bf16[16,32,768]{2,1,0:T(8,128)(2,1)}), bf16[16,32,768]{2,1,0:T(8,128)(2,1)}, u32[]{:S(2)}, u32[]{:S(2)}) async-start(bf16[16,32,768]{2,1,0:T(8,128)(2,1)} %bitcast.58), calls=%async_computation.2 | async-start | bytes 1572864 | tf_op jit(solution)/shard_map/all_to_all | solution.py:399
  193.6 29.0 %collective-permute-start.26 = (bf16[512,1024]{1,0:T(8,128)(2,1)}, bf16[512,1024]{1,0:T(8,128)(2,1)S(1)}, u32[]{:S(2)}, u32[]{:S(2)}) collective-permute-start(bf16[512,1024]{1,0:T(8,128)(2,1)} %collective-permute-done.24.rest_20_), channel_id=1, source_target_pairs={{0,12},{2,14},{4,0},{6,2},{8,4},{10,6},{12,8},{14,10},{1,13},{3,15... | collective-permute-start | bytes 3145736 | tf_op jit(solution)/shard_map/ppermute | solution.py:30
  194.3 37.5 %collective-permute-start.25 = (bf16[512,1024]{1,0:T(8,128)(2,1)}, bf16[512,1024]{1,0:T(8,128)(2,1)S(1)}, u32[]{:S(2)}, u32[]{:S(2)}) collective-permute-start(bf16[512,1024]{1,0:T(8,128)(2,1)} %collective-permute-done.24.rest_20_), channel_id=1, source_target_pairs={{0,2},{2,0},{4,6},{6,4},{8,10},{10,8},{12,14},{14,12},{1,3},{3,1},... | collective-permute-start | bytes 3145736 | tf_op jit(solution)/shard_map/ppermute | solution.py:34
  194.9 36.9 %collective-permute-start.29 = (bf16[512,1024]{1,0:T(8,128)(2,1)}, bf16[512,1024]{1,0:T(8,128)(2,1)S(1)}, u32[]{:S(2)}, u32[]{:S(2)}) collective-permute-start(bf16[512,1024]{1,0:T(8,128)(2,1)} %collective-permute-done.28.rest_22_), channel_id=1, source_target_pairs={{0,4},{2,6},{4,8},{6,10},{8,12},{10,14},{12,0},{14,2},{1,5},{3,7},... | collective-permute-start | bytes 3145736 | tf_op jit(solution)/shard_map/ppermute | solution.py:30
  (33 other events, 571.7 us)

commit v2 on v1

--- a/solution.py
+++ b/solution.py
@@ -18,6 +18,10 @@
 LOG2E = 1.4426950408889634
 
 
+RING = (0, 7, 1, 6, 2, 5, 3, 4)
+PLACES = ((0, 0), (-1, 0), (1, 0), (0, 1), (-1, 1), (1, 1), (2, 0), (2, 1))
+
+
 def sent_to_all(value, axis):
     length = lax.axis_size(axis)
     return lax.all_to_all(
@@ -49,134 +53,142 @@
     found = [((0, 0), 0, shard)]
     for step in range(1, 4):
         up, down = z_shift(up, 1), z_shift(down, -1)
-        found += [((8 - step, step), 0, up), ((step, step), 0, down)]
+        found += [((2 * step - 1, step), 0, up), ((2 * step, step), 0, down)]
     found += [
-        ((4, 4), 0, z_shift(up[:half], 1)),
-        ((4, 4), half, z_shift(down[half:], -1)),
+        ((7, 4), 0, z_shift(up[:half], 1)),
+        ((7, 4), half, z_shift(down[half:], -1)),
     ]
     shards = []
-    for (hop, step), first, value in found:
-        shards.append(((hop, 0, first), value))
-        shards.append(((hop, 1, first), core_swap(value)))
+    for (place, step), first, value in found:
+        shards.append(((place, 0, first), value))
+        shards.append(((place, 1, first), core_swap(value)))
     return shards
 
 
-def mm_kernel(tp_ref, place_ref, sums_ref, gain_ref, *rest, halves, shards, has_acc, last, width):
-    count = len(halves)
-    copies = sum(2 if h else 1 for h in halves)
+def mm_kernel(table_ref, sums_ref, gain_ref, *rest, row, count, shards, has_acc, last, width):
     weights, rest = rest[: len(shards)], rest[len(shards) :]
-    pieces, rest = rest[:copies], rest[copies:]
+    pieces, rest = rest[:count], rest[count:]
     if has_acc:
         acc_in, rest = rest[0], rest[1:]
-    out_ref, xbuf, wbuf, acc, xsem, wsem, asem = rest
-    rows = xbuf.shape[1]
-    half = rows // 2
-    position = 0
-    for p, is_half in enumerate(halves):
-        if is_half:
-            for k in range(2):
-                pltpu.make_async_copy(
-                    pieces[position + k], xbuf.at[p, pl.ds(k * half, half)], xsem.at[p]
-                ).start()
-            position += 2
-        else:
-            pltpu.make_async_copy(pieces[position], xbuf.at[p], xsem.at[p]).start()
-            position += 1
-    for ref, (hop, other, first) in zip(weights, shards):
-        block = place_ref[hop]
-        start = place_ref[8 + other] + first
-
-        def fetch(ref=ref, block=block, start=start):
-            pltpu.make_async_copy(
-                ref,
-                wbuf.at[block, pl.ds(pl.multiple_of(start, 256), ref.shape[0])],
-                wsem.at[block],
-            ).start()
-
-        if count == 8:
-            fetch()
-        else:
-            wanted = tp_ref[0] == block
-            for p in range(1, count):
-                wanted = wanted | (tp_ref[p] == block)
-            pl.when(wanted)(fetch)
+    out_ref, xbuf, wbuf, acc, inverse, high, low, xsem, wsem, asem = rest
+    part = xbuf.shape[1] // 2
+    for p in range(count):
+
+        @pl.when(table_ref[row, 18 + p] > 0)
+        def _(p=p):
+            pltpu.make_async_copy(pieces[p], xbuf.at[p], xsem.at[p]).start()
+
+    for k in range(8):
+        mine = [(ref, key) for ref, key in zip(weights, shards) if key[0] == k]
+        if mine:
+
+            @pl.when(table_ref[row, k] >= 0)
+            def _(k=k, mine=mine):
+                for ref, (_, other, first) in mine:
+                    start = pl.multiple_of(table_ref[row, 16 + other] + first, 256)
+                    pltpu.make_async_copy(
+                        ref, wbuf.at[k, pl.ds(start, ref.shape[0])], wsem.at[k]
+                    ).start()
+
     if has_acc:
         load = pltpu.make_async_copy(acc_in, acc, asem)
         load.start()
     total = jnp.sum(jnp.transpose(sums_ref[...]), axis=1, keepdims=True)
-    inverse = lax.rsqrt(total * (1.0 / width) + norm_eps)
+    inverse[...] = lax.rsqrt(total * (1.0 / width) + norm_eps)
     if has_acc:
         load.wait()
     else:
         acc[...] = jnp.zeros_like(acc)
-
-    def visit(p, carry):
-        block = tp_ref[p]
+    used = table_ref[row, 34]
+    upper, lower = pl.ds(0, part), pl.ds(part, part)
+
+    def ready(i):
+        p = table_ref[row, table_ref[row, 26 + i]]
         pltpu.make_async_copy(xbuf.at[p], xbuf.at[p], xsem.at[p]).wait()
-        pltpu.make_async_copy(wbuf.at[block], wbuf.at[block], wsem.at[block]).wait()
-        gain = gain_ref[pl.ds(block, 1), :]
-        normed = (xbuf[p].astype(jnp.float32) * inverse * gain).astype(jnp.bfloat16)
-        acc[...] += jnp.dot(normed, wbuf[block], preferred_element_type=jnp.float32)
+
+    def normed(i, at):
+        k = table_ref[row, 26 + i]
+        gain = gain_ref[pl.ds(table_ref[row, 8 + k], 1), :]
+        x = xbuf[table_ref[row, k], at, :].astype(jnp.float32)
+        return (x * inverse[at, :] * gain).astype(jnp.bfloat16)
+
+    def visit(i, carry):
+        k = table_ref[row, 26 + i]
+        following = jnp.minimum(i + 1, used - 1)
+        pl.when(i + 1 < used)(lambda: ready(following))
+        pltpu.make_async_copy(wbuf.at[k], wbuf.at[k], wsem.at[k]).wait()
+        low[...] = normed(i, lower)
+        acc[upper, :] += jnp.dot(high[...], wbuf[k], preferred_element_type=jnp.float32)
+        high[...] = normed(following, upper)
+        acc[lower, :] += jnp.dot(low[...], wbuf[k], preferred_element_type=jnp.float32)
         return carry
 
-    lax.fori_loop(0, count, visit, 0)
+    @pl.when(used > 0)
+    def _():
+        ready(0)
+        high[...] = normed(0, upper)
+        lax.fori_loop(0, used, visit, 0)
+
     if last:
         out_ref[...] = acc[...].astype(out_ref.dtype)
     else:
         out_ref[...] = acc[...]
 
 
-def project(tp, place, sums, gain, weights, pieces, acc=None, last=True):
+def project(table, row, sums, gain, weights, pieces, hops=8, acc=None, last=True):
+    weights = [pair for pair in weights if pair[0][0] < hops]
     shards = tuple(key for key, _ in weights)
     weights = [value for _, value in weights]
     blocks, feats = gain.shape
     columns = weights[0].shape[1]
     rows = sums.shape[1]
-    halves = tuple(isinstance(piece, tuple) for piece in pieces)
-    flat = []
-    for piece in pieces:
-        flat.extend(piece if isinstance(piece, tuple) else (piece,))
     count = len(pieces)
     smem = pl.BlockSpec(memory_space=pltpu.SMEM)
     vmem = pl.BlockSpec(memory_space=pltpu.VMEM)
     anyspace = pl.BlockSpec(memory_space=pl.ANY)
     extra = [] if acc is None else [acc]
+    typical = min(count, 4)
     return pl.pallas_call(
         functools.partial(
             mm_kernel,
-            halves=halves,
+            row=row,
+            count=count,
             shards=shards,
             has_acc=acc is not None,
             last=last,
             width=feats * blocks,
         ),
         out_shape=jax.ShapeDtypeStruct((rows, columns), jnp.bfloat16 if last else jnp.float32),
-        in_specs=[smem, smem, vmem, vmem]
-        + [anyspace] * (len(weights) + len(flat) + len(extra)),
+        in_specs=[smem, vmem, vmem] + [anyspace] * (len(weights) + count + len(extra)),
         out_specs=vmem,
         scratch_shapes=[
             pltpu.VMEM((count, rows, feats), jnp.bfloat16),
             pltpu.VMEM((blocks, feats, columns), jnp.bfloat16),
             pltpu.VMEM((rows, columns), jnp.float32),
+            pltpu.VMEM((rows, 1), jnp.float32),
+            pltpu.VMEM((rows // 2, feats), jnp.bfloat16),
+            pltpu.VMEM((rows // 2, feats), jnp.bfloat16),
             pltpu.SemaphoreType.DMA((count,)),
             pltpu.SemaphoreType.DMA((blocks,)),
             pltpu.SemaphoreType.DMA,
         ],
         compiler_params=pltpu.CompilerParams(vmem_limit_bytes=44 << 20),
         cost_estimate=pl.CostEstimate(
-            flops=2 * rows * columns * feats * count,
-            bytes_accessed=2 * count * feats * (rows + columns),
+            flops=2 * rows * columns * feats * typical,
+            bytes_accessed=2 * typical * feats * (rows + columns),
             transcendentals=0,
         ),
         name="project",
-    )(tp, place, sums, gain, *weights, *flat, *extra)
-
-
-def attend_kernel(meta_ref, clen_ref, rows_hbm, cache_ref, score_ref, *rest, seq, has_in):
+    )(table, sums, gain, *weights, *pieces, *extra)
+
+
+def attend_kernel(meta_ref, clen_ref, rows_hbm, cache_hbm, score_ref, *rest, seq, has_in):
     if has_in:
         rest = rest[1:]
-    ctx_ref, value_ref, rows_ref, obuf, rsems, sems = rest
+    ctx_ref, value_ref, rows_ref, cache_ref, obuf, rsems, csem, sems = rest
     steps = rows_ref.shape[0]
+    fill = pltpu.make_async_copy(cache_hbm, cache_ref, csem)
+    fill.start()
     positions = cache_ref.shape[1]
     wide = GROUP * seq
     factor = (HD ** (-0.5)) * LOG2E
@@ -257,6 +269,7 @@
             value_ref[pl.ds(place, 1), :] = jnp.broadcast_to(scored, (1, value_ref.shape[1]))
         return carry
 
+    fill.wait()
     lax.fori_loop(0, steps // together, visit, 0)
     for i in range(steps):
         pltpu.make_async_copy(obuf.at[i], ctx_ref.at[meta_ref[1, i]], sems.at[i]).wait()
@@ -274,12 +287,14 @@
             jax.ShapeDtypeStruct((slots, seq, GROUP * HD), jnp.bfloat16),
             jax.ShapeDtypeStruct((slots, HD), jnp.float32),
         ),
-        in_specs=[smem, smem, anyspace, vmem, vmem] + [anyspace] * len(extra),
+        in_specs=[smem, smem, anyspace, anyspace, vmem] + [anyspace] * len(extra),
         out_specs=(anyspace, vmem),
         scratch_shapes=[
             pltpu.VMEM(rows.shape, jnp.bfloat16),
+            pltpu.VMEM(cache.shape, jnp.bfloat16),
             pltpu.VMEM((steps, seq, GROUP * HD), jnp.bfloat16),
             pltpu.SemaphoreType.DMA((steps // 4,)),
+            pltpu.SemaphoreType.DMA,
             pltpu.SemaphoreType.DMA((steps,)),
         ],
         input_output_aliases={} if earlier is None else {5: 0},
@@ -306,14 +321,6 @@
     rows = peers * seq
 
     weights = ring_weights(qkv_weight[0])
-    z, core = me // 2, me % 2
-    place = jnp.concatenate(
-        [
-            (z + jnp.arange(8, dtype=jnp.int32)) % 8,
-            jnp.stack([core, 1 - core]) * qkv_weight.shape[1],
-        ]
-    ).astype(jnp.int32)
-
     leaves = leaf_of_step.reshape(peers, steps_here)
     lengths = step_len.reshape(peers, steps_here)
     index = jnp.arange(steps_here, dtype=jnp.int32)
@@ -364,45 +371,66 @@
     squares = [
         jnp.sum(jnp.square(part.astype(jnp.float32)), axis=1) for part in (a, b)
     ]
-    sums = sent_to_all(jnp.concatenate(squares), "tensor")
+
+    y, h, z, core = tensor // 2, tensor % 2, me // 2, me % 2
+    block = (z + jnp.array(RING, jnp.int32)) % 8
+    owner = (y + jnp.array([dy for dy, _ in PLACES], jnp.int32)) % 4 * 2 + (
+        h + jnp.array([dx for _, dx in PLACES], jnp.int32)
+    ) % 2
+    meets = owner[None, :] == block[:, None]
+    start = jnp.stack([core, 1 - core]) * qkv_weight.shape[1]
+    ring = jnp.arange(8, dtype=jnp.int32)
+
+    def table_row(inside, allowed):
+        local = [inside.index(p) if p in inside else -1 for p in range(8)]
+        use = meets & allowed & jnp.array([v >= 0 for v in local])[None, :]
+        which = jnp.sum(jnp.where(use, jnp.array(local, jnp.int32)[None, :] + 1, 0), axis=1) - 1
+        used = jnp.sum(which[:, None] == ring[None, :], axis=0)
+        place = jnp.cumsum(which >= 0) - 1
+        order = jnp.sum(
+            jnp.where((place[:, None] == ring[None, :]) & (which >= 0)[:, None], ring[:, None], 0),
+            axis=0,
+        )
+        total = jnp.sum(which >= 0)[None]
+        return jnp.concatenate([which, block, start, used, order, total]).astype(jnp.int32)
+
+    sooner = (ring < 7)[:, None]
+    a_soon, b_soon = (0, 1, 2, 3, 5, 6), (0, 1, 2, 3)
+    whole = tuple(range(8))
+    in_a = jnp.array([p in a_soon for p in whole])[None, :]
+    in_b = jnp.array([p in b_soon for p in whole])[None, :]
+    table = jnp.stack(
+        [
+            table_row(a_soon, sooner),
+            table_row(whole, ~(sooner & in_a)),
+            table_row(b_soon, sooner),
+            table_row(whole, ~(sooner & in_b)),
+        ]
+    )
+    gain = norm_gain[0].reshape(-1, feats)
+    squares, table, meta, gain = lax.optimization_barrier(
+        (jnp.concatenate(squares), table, (meta[:, :peers], meta[:, peers:]), gain)
+    )
+    sums = sent_to_all(squares, "tensor")
     sums_a, sums_b = sums[:, :rows], sums[:, rows:]
-
-    y, h = tensor // 2, tensor % 2
-
-    def owner(dy, dx):
-        return ((y + dy) % 4) * 2 + ((h + dx) % 2)
-
-    first = [owner(0, 0), owner(-1, 0), owner(1, 0), owner(0, 1), owner(-1, 1)]
-    then = [owner(1, 1), owner(2, 0), owner(2, 1)]
-    gain = norm_gain[0].reshape(-1, feats)
-    out_a = project(
-      jnp.stack(first + then).astype(jnp.int32),
-      place,
-      sums_a,
-      gain,
-      weights,
-      [a, a_left, a_right, a_x, ax_left, ax_right, a_far, ax_far],
+    all_a = [a, a_left, a_right, a_x, ax_left, ax_right, a_far, ax_far]
+    all_b = [b, b_left, b_right, b_x, bx_left, bx_right, b_far, bx_far]
+    part_a = project(
+        table, 0, sums_a, gain, weights, [all_a[p] for p in a_soon], hops=7, last=False
     )
     part_b = project(
-      jnp.stack(first).astype(jnp.int32),
-      place,
-      sums_b,
-      gain,
-      weights,
-      [b, b_left, b_right, b_x, bx_left],
-      last=False,
-    )
-    out_b = project(
-        jnp.stack(then).astype(jnp.int32), place, sums_b, gain, weights, [bx_right, b_far, bx_far], acc=part_b
-    )
+        table, 2, sums_b, gain, weights, [all_b[p] for p in b_soon], hops=7, last=False
+    )
+    out_a = project(table, 1, sums_a, gain, weights, all_a, acc=part_a)
+    out_b = project(table, 3, sums_b, gain, weights, all_b, acc=part_b)
 
     out_a = lax.all_to_all(out_a.reshape(peers, seq, -1), "dp", 0, 0, tiled=True)
     out_b = out_b.reshape(peers, seq, -1)
     cache = caches[0]
     score = score_weight[0].reshape(GROUP, HD)
-    context, value_b = attend(meta[:, peers:], cache_len, out_b, cache, score, steps_here)
+    context, value_b = attend(meta[1], cache_len, out_b, cache, score, steps_here)
     context, value_a = attend(
-        meta[:, :peers], cache_len, out_a, cache, score, steps_here, earlier=context
+        meta[0], cache_len, out_a, cache, score, steps_here, earlier=context
     )
     contexts = context.reshape(1, leaves_here, per_leaf, seq, GROUP * HD)
     model_weight = jnp.where(lax.axis_index("mp") == 0, prior_weight, 1.0).astype(jnp.float32)

time: 270 us -> 262 us (0.970); the launches traced: 265 us -> 260 us
  waiting for transfers between devices: 112 us -> 65.6 us
  blocking collectives: 8.99 us -> 46.2 us
  starting transfers between devices: 76.1 us -> 70.2 us
  Pallas kernels: 42.2 us -> 47.5 us
  other arithmetic: 4.65 us -> 8.75 us
    all_to_all x1 -> x2, blocking collectives: 8.99 us -> 46.2 us  [sent_to_all(): lax.all_to_all(jnp.broadcast_to(value[None], (length, *value.shape)), axi...]
    ppermute x10, waiting for transfers between devices: 47.5 us -> 18 us  [y_shift(): return lax.ppermute(value, 'tensor', pairs)]
    ppermute x8, waiting for transfers between devices: 35.6 us -> 26.7 us  [z_shift(): return lax.ppermute(value, 'dp', pairs)]
    all_to_all x1, starting transfers between devices: 11.1 us -> 5.44 us  [staged(): lax.all_to_all(out_a.reshape(peers, seq, -1), 'dp', 0, 0, tiled=True)]
    pallas_call x3 -> x4, Pallas kernels: 29.5 us -> 34.9 us  [project(): pl.pallas_call(functools.partial(mm_kernel, row=row, count=count, shards=...]
    all_to_all x1 -> x0, waiting for transfers between devices: 5.12 us -> none  [sent_to_all(): lax.all_to_all(jnp.broadcast_to(value[None], (length, *value.shape)), axi...]
    ppermute x4, starting transfers between devices: 6.37 us -> 11.2 us  [x_swap(): return lax.ppermute(value, 'tensor', [(t, t ^ 1) for t in range(8)])]
    ppermute x9, starting transfers between devices: 20.5 us -> 16.3 us  [core_swap(): return lax.ppermute(value, 'dp', [(d, d ^ 1) for d in range(16)])]
  transfers between devices with their start and end apart: 34 -> 33, of which waited for: 13 -> 11; matrix products, arithmetic and copies ran while one was open for 4% -> 7% of each run, Pallas kernels for 14% -> 16%
where the time goes in v2:
time: 262 us; the launch traced here: 260 us
  starting transfers between devices  70.2 us (27%)
  waiting for transfers between devices  65.6 us (25%)
  Pallas kernels  47.5 us (18%)
  blocking collectives  46.2 us (18%)
  local copies, waits for them, and re-layouts  21 us (8%)
  other arithmetic  8.75 us (3%)
    all_to_all x2, blocking collectives, sent_to_all(): lax.all_to_all(jnp.broadcast_to(value[None], (length, *value.shape)), axi...  46.2 us
    pallas_call x4, Pallas kernels, project(): pl.pallas_call(functools.partial(mm_kernel, row=row, count=count, shards=...  34.9 us
    ppermute x8, waiting for transfers between devices, z_shift(): return lax.ppermute(value, 'dp', pairs)  26.7 us
    ppermute x4, waiting for transfers between devices, x_swap(): return lax.ppermute(value, 'tensor', [(t, t ^ 1) for t in range(8)])  20.5 us
    ppermute x10, waiting for transfers between devices, y_shift(): return lax.ppermute(value, 'tensor', pairs)  18 us
    ppermute x9, starting transfers between devices, core_swap(): return lax.ppermute(value, 'dp', [(d, d ^ 1) for d in range(16)])  16.3 us
    ppermute x8, starting transfers between devices, z_shift(): return lax.ppermute(value, 'dp', pairs)  16.2 us
    ppermute x10, starting transfers between devices, y_shift(): return lax.ppermute(value, 'tensor', pairs)  14.6 us
  transfers between devices with their start and end apart: 33, of which 11 were waited for; matrix products, arithmetic and copies ran while one was open for 7% of the time, Pallas kernels for 16%

profile of v2, /device:TPU:1, one launch (start us, length us, event | category | flops | bytes accessed | tf_op | source)
XLA Modules:
  0.0 260.5 jit_solution(10628746537547636828)
XLA Ops:
  3.2 4.0 %collective-permute-start.3 = (bf16[512,768]{1,0:T(8,128)(2,1)}, bf16[512,768]{1,0:T(8,128)(2,1)}, u32[]{:S(2)}, u32[]{:S(2)}) collective-permute-start(bf16[512,768]{1,0:T(8,128)(2,1)} %bitcast.67), channel_id=1, source_target_pairs={{0,224},{16,240},{32,0},{48,16},{64,32},{80,48},{96,64},{112,80},{... | collective-permute-start | bytes 2359304 | tf_op jit(solution)/shard_map/ppermute | solution.py:43
  10.9 2.7 %collective-permute-start.19 = (bf16[512,1024]{1,0:T(8,128)(2,1)}, bf16[512,1024]{1,0:T(8,128)(2,1)}, u32[]{:S(2)}, u32[]{:S(2)}) collective-permute-start(bf16[512,1024]{1,0:T(8,128)(2,1)} %bitcast.79), channel_id=1, source_target_pairs={{0,2},{2,0},{4,6},{6,4},{8,10},{10,8},{12,14},{14,12},{1,3},{3,1},... | collective-permute-start | bytes 3145736 | tf_op jit(solution)/shard_map/ppermute | solution.py:38
  16.6 6.5 %all-to-all-start = ((bf16[16,32,1024]{2,1,0:T(8,128)(2,1)}), bf16[16,32,1024]{2,1,0:T(8,128)(2,1)}, u32[]{:S(2)}, u32[]{:S(2)}) async-start(bf16[16,32,1024]{2,1,0:T(8,128)(2,1)} %gather_fusion.1), calls=%async_computation | async-start | bytes 2097152 | tf_op jit(solution)/shard_map/all_to_all | solution.py:338
  31.6 5.9 %collective-permute-done.19.rest_17_.rest_21_ = bf16[512,1024]{1,0:T(8,128)(2,1)} collective-permute-done((bf16[512,1024]{1,0:T(8,128)(2,1)}, bf16[512,1024]{1,0:T(8,128)(2,1)}, u32[]{:S(2)}, u32[]{:S(2)}) %collective-permute-start.19) | collective-permute-done | bytes 1048608 | tf_op jit(solution)/shard_map/ppermute | solution.py:38
  41.2 9.2 %collective-permute-done.18.rest_16_.rest_20_ = bf16[512,1024]{1,0:T(8,128)(2,1)} collective-permute-done((bf16[512,1024]{1,0:T(8,128)(2,1)}, bf16[512,1024]{1,0:T(8,128)(2,1)}, u32[]{:S(2)}, u32[]{:S(2)}) %collective-permute-start.18) | collective-permute-done | bytes 1048608 | tf_op jit(solution)/shard_map/ppermute | solution.py:34
  51.9 14.0 %collective-permute-done.5.rest_6_ = bf16[512,768]{1,0:T(8,128)(2,1)} collective-permute-done((bf16[512,768]{1,0:T(8,128)(2,1)}, bf16[512,768]{1,0:T(8,128)(2,1)}, u32[]{:S(2)}, u32[]{:S(2)}) %collective-permute-start.5) | collective-permute-done | bytes 786464 | tf_op jit(solution)/shard_map/ppermute | solution.py:43
  75.4 5.4 %collective-permute-start.8 = (bf16[512,768]{1,0:T(8,128)(2,1)}, bf16[512,768]{1,0:T(8,128)(2,1)}, u32[]{:S(2)}, u32[]{:S(2)}) collective-permute-start(bf16[512,768]{1,0:T(8,128)(2,1)} %collective-permute-done.7.rest_8_), channel_id=1, source_target_pairs={{0,16},{16,0},{32,48},{48,32},{64,80},{80,64},{96,112},{112,96},{1... | collective-permute-start | bytes 2359304 | tf_op jit(solution)/shard_map/ppermute | solution.py:47
  81.3 6.5 %collective-permute-done.9.rest_10_ = bf16[512,768]{1,0:T(8,128)(2,1)S(1)} collective-permute-done((bf16[512,768]{1,0:T(8,128)(2,1)}, bf16[512,768]{1,0:T(8,128)(2,1)S(1)}, u32[]{:S(2)}, u32[]{:S(2)}) %collective-permute-start.9) | collective-permute-done | bytes 786464 | tf_op jit(solution)/shard_map/ppermute | solution.py:43
  91.3 4.8 %collective-permute-done.20.rest_22_ = bf16[512,1024]{1,0:T(8,128)(2,1)} collective-permute-done((bf16[512,1024]{1,0:T(8,128)(2,1)}, bf16[512,1024]{1,0:T(8,128)(2,1)}, u32[]{:S(2)}, u32[]{:S(2)}) %collective-permute-start.20) | collective-permute-done | bytes 1048608 | tf_op jit(solution)/shard_map/ppermute | solution.py:34
  98.3 5.9 %collective-permute-start.10 = (bf16[512,768]{1,0:T(8,128)(2,1)S(1)}, bf16[512,768]{1,0:T(8,128)(2,1)}, u32[]{:S(2)}, u32[]{:S(2)}) collective-permute-start(bf16[512,768]{1,0:T(8,128)(2,1)S(1)} %collective-permute-done.9.rest_10_), channel_id=1, source_target_pairs={{0,16},{16,0},{32,48},{48,32},{64,80},{80,64},{96,112},{112,96},{1... | collective-permute-start | bytes 2359304 | tf_op jit(solution)/shard_map/ppermute | solution.py:47
  113.9 6.2 %collective-permute-done.15.rest_16_ = bf16[256,768]{1,0:T(8,128)(2,1)} collective-permute-done((bf16[256,768]{1,0:T(8,128)(2,1)S(1)}, bf16[256,768]{1,0:T(8,128)(2,1)}, u32[]{:S(2)}, u32[]{:S(2)}) %collective-permute-start.15) | collective-permute-done | bytes 393248 | tf_op jit(solution)/shard_map/ppermute | solution.py:43
  125.7 33.5 %all_to_all.24 = f32[8,1,1024]{2,1,0:T(1,128)S(1)} all-to-all(f32[8,1,1024]{2,1,0:T(1,128)S(1)} %broadcast_in_dim.206), channel_id=1, replica_groups=mesh['dp'=16,'tensor'=8,'mp'=2] {'tensor'}, dimensions={0} | all-to-all | bytes 65536 | tf_op jit(solution)/shard_map/all_to_all | solution.py:27
  164.4 9.3 %project.4.rest_26_ = f32[512,768]{1,0:T(8,128)} custom-call(s32[4,35]{1,0:T(4,128)S(1)} %pad_add_fusion.1.table_ref, f32[8,512]{1,0:T(8,128)S(1)} %get-tuple-element.34.sums_ref, f32[8,1024]{1,0:T(8,128)S(1)} %reshape_squeeze.7.gain_ref, bf16[512,768]{1,0:T(8,128)(2,1)S(1)} %bitcast.69, bf16[512,768]{1,0:T(8,128)(2,1)S(1)} %copy-done.6, ...), custom_call_target="tpu_custom_call" | custom-call | flops 3221225472 | bytes 10485760 | tf_op jit(solution)/shard_map/project/pallas_call | solution.py:151
  173.7 3.8 %collective-permute-start.26 = (bf16[512,1024]{1,0:T(8,128)(2,1)}, bf16[512,1024]{1,0:T(8,128)(2,1)}, u32[]{:S(2)}, u32[]{:S(2)}) collective-permute-start(bf16[512,1024]{1,0:T(8,128)(2,1)} %bitcast.33.rest_14_.rest_18_), channel_id=1, source_target_pairs={{0,2},{2,0},{4,6},{6,4},{8,10},{10,8},{12,14},{14,12},{1,3},{3,1},... | collective-permute-start | bytes 3145736 | tf_op jit(solution)/shard_map/ppermute | solution.py:38
  177.5 7.9 %project.5 = bf16[512,768]{1,0:T(8,128)(2,1)S(1)} custom-call(s32[4,35]{1,0:T(4,128)S(1)} %pad_add_fusion.1.table_ref, f32[8,512]{1,0:T(8,128)S(1)} %get-tuple-element.34.sums_ref, f32[8,1024]{1,0:T(8,128)S(1)} %reshape_squeeze.7.gain_ref, bf16[512,768]{1,0:T(8,128)(2,1)S(1)} %bitcast.70, bf16[512,768]{1,0:T(8,128)(2,1)S(1)} %copy-done.6, ...), custom_call_target="tpu_custom_call" | custom-call | flops 3221225472 | bytes 10485760 | tf_op jit(solution)/shard_map/project/pallas_call | solution.py:151
  186.3 5.4 %all-to-all-start.2 = ((bf16[16,32,768]{2,1,0:T(8,128)(2,1)}), bf16[16,32,768]{2,1,0:T(8,128)(2,1)}, u32[]{:S(2)}, u32[]{:S(2)}) async-start(bf16[16,32,768]{2,1,0:T(8,128)(2,1)} %bitcast.73), calls=%async_computation.2 | async-start | bytes 1572864 | tf_op jit(solution)/shard_map/all_to_all | solution.py:427
  194.2 2.8 %collective-permute-start.29 = (bf16[512,1024]{1,0:T(8,128)(2,1)}, bf16[512,1024]{1,0:T(8,128)(2,1)}, u32[]{:S(2)}, u32[]{:S(2)}) collective-permute-start(bf16[512,1024]{1,0:T(8,128)(2,1)} %collective-permute-done.25.rest_16_.rest_20_), channel_id=1, source_target_pairs={{0,12},{2,14},{4,0},{6,2},{8,4},{10,6},{12,8},{14,10},{1,13},{3,15... | collective-permute-start | bytes 3145736 | tf_op jit(solution)/shard_map/ppermute | solution.py:34
  197.0 3.9 %collective-permute-done.26.rest_17_.rest_21_ = bf16[512,1024]{1,0:T(8,128)(2,1)} collective-permute-done((bf16[512,1024]{1,0:T(8,128)(2,1)}, bf16[512,1024]{1,0:T(8,128)(2,1)}, u32[]{:S(2)}, u32[]{:S(2)}) %collective-permute-start.26) | collective-permute-done | bytes 1048608 | tf_op jit(solution)/shard_map/ppermute | solution.py:38
  204.3 8.2 %project.6.rest_26_ = f32[512,768]{1,0:T(8,128)} custom-call(s32[4,35]{1,0:T(4,128)S(1)} %pad_add_fusion.1.table_ref, f32[8,512]{1,0:T(8,128)S(1)} %get-tuple-element.33.sums_ref, f32[8,1024]{1,0:T(8,128)S(1)} %reshape_squeeze.7.gain_ref, bf16[512,768]{1,0:T(8,128)(2,1)S(1)} %bitcast.71, bf16[512,768]{1,0:T(8,128)(2,1)S(1)} %copy-done.7, ...), custom_call_target="tpu_custom_call" | custom-call | flops 3221225472 | bytes 10485760 | tf_op jit(solution)/shard_map/project/pallas_call | solution.py:151
  212.6 10.8 %collective-permute-done.28.rest_23_ = bf16[512,1024]{1,0:T(8,128)(2,1)} collective-permute-done((bf16[512,1024]{1,0:T(8,128)(2,1)}, bf16[512,1024]{1,0:T(8,128)(2,1)}, u32[]{:S(2)}, u32[]{:S(2)}) %collective-permute-start.28) | collective-permute-done | bytes 1048608 | tf_op jit(solution)/shard_map/ppermute | solution.py:38
  223.4 9.5 %project.7 = bf16[512,768]{1,0:T(8,128)(2,1)S(1)} custom-call(s32[4,35]{1,0:T(4,128)S(1)} %pad_add_fusion.1.table_ref, f32[8,512]{1,0:T(8,128)S(1)} %get-tuple-element.33.sums_ref, f32[8,1024]{1,0:T(8,128)S(1)} %reshape_squeeze.7.gain_ref, bf16[512,768]{1,0:T(8,128)(2,1)S(1)} %bitcast.72, bf16[512,768]{1,0:T(8,128)(2,1)S(1)} %copy-done.7, ...), custom_call_target="tpu_custom_call" | custom-call | flops 3221225472 | bytes 10485760 | tf_op jit(solution)/shard_map/project/pallas_call | solution.py:151
  232.9 6.4 %attend.2 = (bf16[32,32,512]{2,1,0:T(8,128)(2,1)}, f32[32,128]{1,0:T(8,128)S(1)}) custom-call(s32[3,16]{1,0:T(4,128)S(1)} %get-tuple-element.15.meta_ref, s32[4]{0:T(128)S(1)} %copy-done.19, bf16[16,32,768]{2,1,0:T(8,128)(2,1)S(1)} %bitcast.76, bf16[4,768,256]{2,1,0:T(8,128)(2,1)S(1)} %bitcast.74, f32[4,128]{1,0:T(4,128)S(1)} %bitcast.77), custom_call_target="tpu_custom_call" | custom-call | flops 805306368 | bytes 3407872 | tf_op jit(solution)/shard_map/attend/pallas_call | solution.py:284
  240.7 6.3 %attend.3 = (bf16[32,32,512]{2,1,0:T(8,128)(2,1)}, f32[32,128]{1,0:T(8,128)S(1)}) custom-call(s32[3,16]{1,0:T(4,128)S(1)} %get-tuple-element.11.meta_ref, s32[4]{0:T(128)S(1)} %copy-done.19, bf16[16,32,768]{2,1,0:T(8,128)(2,1)} %all-to-all-done.2.rows_hbm, bf16[4,768,256]{2,1,0:T(8,128)(2,1)S(1)} %bitcast.75, ...), custom_call_target="tpu_custom_call", output_to_operand_aliasing={{0}: (5, {})} | custom-call | flops 805306368 | bytes 3407872 | tf_op jit(solution)/shard_map/attend/pallas_call | solution.py:284
  247.2 12.7 %all_to_all.25 = f32[16,4,8]{2,1,0:T(4,128)S(1)} all-to-all(f32[16,4,8]{2,1,0:T(4,128)S(1)} %broadcast_in_dim.207), channel_id=1, replica_groups=mesh['dp'=16,'tensor'=8,'mp'=2] {'tensor','mp'}, dimensions={0} | all-to-all | bytes 4096 | tf_op jit(solution)/shard_map/all_to_all | solution.py:27
  (190 shorter events, 67.7 us)
Async XLA Ops:
  0.6 25.0 %collective-permute-start.1 = (bf16[512,768]{1,0:T(8,128)(2,1)}, bf16[512,768]{1,0:T(8,128)(2,1)}, u32[]{:S(2)}, u32[]{:S(2)}) collective-permute-start(bf16[512,768]{1,0:T(8,128)(2,1)} %bitcast.66), channel_id=1, source_target_pairs={{0,32},{16,48},{32,64},{48,80},{64,96},{80,112},{96,128},{112,144}... | collective-permute-start | bytes 2359304 | tf_op jit(solution)/shard_map/ppermute | solution.py:43
  10.9 26.5 %collective-permute-start.19 = (bf16[512,1024]{1,0:T(8,128)(2,1)}, bf16[512,1024]{1,0:T(8,128)(2,1)}, u32[]{:S(2)}, u32[]{:S(2)}) collective-permute-start(bf16[512,1024]{1,0:T(8,128)(2,1)} %bitcast.79), channel_id=1, source_target_pairs={{0,2},{2,0},{4,6},{6,4},{8,10},{10,8},{12,14},{14,12},{1,3},{3,1},... | collective-permute-start | bytes 3145736 | tf_op jit(solution)/shard_map/ppermute | solution.py:38
  13.6 26.1 %collective-permute-start.17 = (bf16[512,1024]{1,0:T(8,128)(2,1)}, bf16[512,1024]{1,0:T(8,128)(2,1)}, u32[]{:S(2)}, u32[]{:S(2)}) collective-permute-start(bf16[512,1024]{1,0:T(8,128)(2,1)} %bitcast.80), channel_id=1, source_target_pairs={{0,4},{2,6},{4,8},{6,10},{8,12},{10,14},{12,0},{14,2},{1,5},{3,7},... | collective-permute-start | bytes 3145736 | tf_op jit(solution)/shard_map/ppermute | solution.py:34
  16.6 64.7 %all-to-all-start = ((bf16[16,32,1024]{2,1,0:T(8,128)(2,1)}), bf16[16,32,1024]{2,1,0:T(8,128)(2,1)}, u32[]{:S(2)}, u32[]{:S(2)}) async-start(bf16[16,32,1024]{2,1,0:T(8,128)(2,1)} %gather_fusion.1), calls=%async_computation | async-start | bytes 2097152 | tf_op jit(solution)/shard_map/all_to_all | solution.py:338
  28.0 38.0 %collective-permute-start.5 = (bf16[512,768]{1,0:T(8,128)(2,1)}, bf16[512,768]{1,0:T(8,128)(2,1)}, u32[]{:S(2)}, u32[]{:S(2)}) collective-permute-start(bf16[512,768]{1,0:T(8,128)(2,1)} %collective-permute-done.1.rest_2_), channel_id=1, source_target_pairs={{0,32},{16,48},{32,64},{48,80},{64,96},{80,112},{96,128},{112,144}... | collective-permute-start | bytes 2359304 | tf_op jit(solution)/shard_map/ppermute | solution.py:43
  29.8 37.3 %collective-permute-start.7 = (bf16[512,768]{1,0:T(8,128)(2,1)}, bf16[512,768]{1,0:T(8,128)(2,1)}, u32[]{:S(2)}, u32[]{:S(2)}) collective-permute-start(bf16[512,768]{1,0:T(8,128)(2,1)} %collective-permute-done.3.rest_4_), channel_id=1, source_target_pairs={{0,224},{16,240},{32,0},{48,16},{64,32},{80,48},{96,64},{112,80},{... | collective-permute-start | bytes 2359304 | tf_op jit(solution)/shard_map/ppermute | solution.py:43
  37.4 29.9 %collective-permute-start.2 = (bf16[512,768]{1,0:T(8,128)(2,1)}, bf16[512,768]{1,0:T(8,128)(2,1)}, u32[]{:S(2)}, u32[]{:S(2)}) collective-permute-start(bf16[512,768]{1,0:T(8,128)(2,1)} %collective-permute-done.1.rest_2_), channel_id=1, source_target_pairs={{0,16},{16,0},{32,48},{48,32},{64,80},{80,64},{96,112},{112,96},{1... | collective-permute-start | bytes 2359304 | tf_op jit(solution)/shard_map/ppermute | solution.py:47
  39.8 33.0 %collective-permute-start.21 = (bf16[512,1024]{1,0:T(8,128)(2,1)}, bf16[512,1024]{1,0:T(8,128)(2,1)}, u32[]{:S(2)}, u32[]{:S(2)}) collective-permute-start(bf16[512,1024]{1,0:T(8,128)(2,1)} %collective-permute-done.19.rest_17_.rest_21_), channel_id=1, source_target_pairs={{0,12},{2,14},{4,0},{6,2},{8,4},{10,6},{12,8},{14,10},{1,13},{3,15... | collective-permute-start | bytes 3145736 | tf_op jit(solution)/shard_map/ppermute | solution.py:34
  50.3 25.0 %collective-permute-start.22 = (bf16[512,1024]{1,0:T(8,128)(2,1)}, bf16[512,1024]{1,0:T(8,128)(2,1)}, u32[]{:S(2)}, u32[]{:S(2)}) collective-permute-start(bf16[512,1024]{1,0:T(8,128)(2,1)} %collective-permute-done.17.rest_15_.rest_19_), channel_id=1, source_target_pairs={{0,4},{2,6},{4,8},{6,10},{8,12},{10,14},{12,0},{14,2},{1,5},{3,7},... | collective-permute-start | bytes 3145736 | tf_op jit(solution)/shard_map/ppermute | solution.py:34
  67.3 28.8 %collective-permute-start.20 = (bf16[512,1024]{1,0:T(8,128)(2,1)}, bf16[512,1024]{1,0:T(8,128)(2,1)}, u32[]{:S(2)}, u32[]{:S(2)}) collective-permute-start(bf16[512,1024]{1,0:T(8,128)(2,1)} %collective-permute-done.19.rest_17_.rest_21_), channel_id=1, source_target_pairs={{0,4},{2,6},{4,8},{6,10},{8,12},{10,14},{12,0},{14,2},{1,5},{3,7},... | collective-permute-start | bytes 3145736 | tf_op jit(solution)/shard_map/ppermute | solution.py:34
  69.9 34.3 %collective-permute-start.6 = (bf16[512,768]{1,0:T(8,128)(2,1)}, bf16[512,768]{1,0:T(8,128)(2,1)}, u32[]{:S(2)}, u32[]{:S(2)}) collective-permute-start(bf16[512,768]{1,0:T(8,128)(2,1)} %collective-permute-done.5.rest_6_), channel_id=1, source_target_pairs={{0,16},{16,0},{32,48},{48,32},{64,80},{80,64},{96,112},{112,96},{1... | collective-permute-start | bytes 2359304 | tf_op jit(solution)/shard_map/ppermute | solution.py:47
  72.8 25.5 %collective-permute-start.11 = (bf16[512,768]{1,0:T(8,128)(2,1)}, bf16[512,768]{1,0:T(8,128)(2,1)}, u32[]{:S(2)}, u32[]{:S(2)}) collective-permute-start(bf16[512,768]{1,0:T(8,128)(2,1)} %collective-permute-done.7.rest_8_), channel_id=1, source_target_pairs={{0,224},{16,240},{32,0},{48,16},{64,32},{80,48},{96,64},{112,80},{... | collective-permute-start | bytes 2359304 | tf_op jit(solution)/shard_map/ppermute | solution.py:43
  75.4 34.3 %collective-permute-start.8 = (bf16[512,768]{1,0:T(8,128)(2,1)}, bf16[512,768]{1,0:T(8,128)(2,1)}, u32[]{:S(2)}, u32[]{:S(2)}) collective-permute-start(bf16[512,768]{1,0:T(8,128)(2,1)} %collective-permute-done.7.rest_8_), channel_id=1, source_target_pairs={{0,16},{16,0},{32,48},{48,32},{64,80},{80,64},{96,112},{112,96},{1... | collective-permute-start | bytes 2359304 | tf_op jit(solution)/shard_map/ppermute | solution.py:47
  87.8 34.0 %collective-permute-start.24 = (bf16[512,1024]{1,0:T(8,128)(2,1)}, bf16[512,1024]{1,0:T(8,128)(2,1)}, u32[]{:S(2)}, u32[]{:S(2)}) collective-permute-start(bf16[512,1024]{1,0:T(8,128)(2,1)} %bitcast.33.rest_14_.rest_18_), channel_id=1, source_target_pairs={{0,4},{2,6},{4,8},{6,10},{8,12},{10,14},{12,0},{14,2},{1,5},{3,7},... | collective-permute-start | bytes 3145736 | tf_op jit(solution)/shard_map/ppermute | solution.py:34
  98.3 60.9 %collective-permute-start.10 = (bf16[512,768]{1,0:T(8,128)(2,1)S(1)}, bf16[512,768]{1,0:T(8,128)(2,1)}, u32[]{:S(2)}, u32[]{:S(2)}) collective-permute-start(bf16[512,768]{1,0:T(8,128)(2,1)S(1)} %collective-permute-done.9.rest_10_), channel_id=1, source_target_pairs={{0,16},{16,0},{32,48},{48,32},{64,80},{80,64},{96,112},{112,96},{1... | collective-permute-start | bytes 2359304 | tf_op jit(solution)/shard_map/ppermute | solution.py:47
  104.2 56.7 %collective-permute-start.12 = (bf16[512,768]{1,0:T(8,128)(2,1)}, bf16[512,768]{1,0:T(8,128)(2,1)}, u32[]{:S(2)}, u32[]{:S(2)}) collective-permute-start(bf16[512,768]{1,0:T(8,128)(2,1)} %collective-permute-done.11.rest_12_), channel_id=1, source_target_pairs={{0,16},{16,0},{32,48},{48,32},{64,80},{80,64},{96,112},{112,96},{1... | collective-permute-start | bytes 2359304 | tf_op jit(solution)/shard_map/ppermute | solution.py:47
  112.0 61.6 %collective-permute-start.23 = (bf16[512,1024]{1,0:T(8,128)(2,1)}, bf16[512,1024]{1,0:T(8,128)(2,1)}, u32[]{:S(2)}, u32[]{:S(2)}) collective-permute-start(bf16[512,1024]{1,0:T(8,128)(2,1)} %collective-permute-done.21.rest_18_.rest_23_), channel_id=1, source_target_pairs={{0,12},{2,14},{4,0},{6,2},{8,4},{10,6},{12,8},{14,10},{1,13},{3,15... | collective-permute-start | bytes 3145736 | tf_op jit(solution)/shard_map/ppermute | solution.py:34
  120.2 71.6 %collective-permute-start.25 = (bf16[512,1024]{1,0:T(8,128)(2,1)}, bf16[512,1024]{1,0:T(8,128)(2,1)}, u32[]{:S(2)}, u32[]{:S(2)}) collective-permute-start(bf16[512,1024]{1,0:T(8,128)(2,1)} %bitcast.33.rest_14_.rest_18_), channel_id=1, source_target_pairs={{0,12},{2,14},{4,0},{6,2},{8,4},{10,6},{12,8},{14,10},{1,13},{3,15... | collective-permute-start | bytes 3145736 | tf_op jit(solution)/shard_map/ppermute | solution.py:34
  121.8 75.2 %collective-permute-start.27 = (bf16[512,1024]{1,0:T(8,128)(2,1)}, bf16[512,1024]{1,0:T(8,128)(2,1)}, u32[]{:S(2)}, u32[]{:S(2)}) collective-permute-start(bf16[512,1024]{1,0:T(8,128)(2,1)} %collective-permute-done.24.rest_15_.rest_19_), channel_id=1, source_target_pairs={{0,2},{2,0},{4,6},{6,4},{8,10},{10,8},{12,14},{14,12},{1,3},{3,1},... | collective-permute-start | bytes 3145736 | tf_op jit(solution)/shard_map/ppermute | solution.py:38
  173.7 27.3 %collective-permute-start.26 = (bf16[512,1024]{1,0:T(8,128)(2,1)}, bf16[512,1024]{1,0:T(8,128)(2,1)}, u32[]{:S(2)}, u32[]{:S(2)}) collective-permute-start(bf16[512,1024]{1,0:T(8,128)(2,1)} %bitcast.33.rest_14_.rest_18_), channel_id=1, source_target_pairs={{0,2},{2,0},{4,6},{6,4},{8,10},{10,8},{12,14},{14,12},{1,3},{3,1},... | collective-permute-start | bytes 3145736 | tf_op jit(solution)/shard_map/ppermute | solution.py:38
  186.3 53.0 %all-to-all-start.2 = ((bf16[16,32,768]{2,1,0:T(8,128)(2,1)}), bf16[16,32,768]{2,1,0:T(8,128)(2,1)}, u32[]{:S(2)}, u32[]{:S(2)}) async-start(bf16[16,32,768]{2,1,0:T(8,128)(2,1)} %bitcast.73), calls=%async_computation.2 | async-start | bytes 1572864 | tf_op jit(solution)/shard_map/all_to_all | solution.py:427
  191.8 31.6 %collective-permute-start.28 = (bf16[512,1024]{1,0:T(8,128)(2,1)}, bf16[512,1024]{1,0:T(8,128)(2,1)}, u32[]{:S(2)}, u32[]{:S(2)}) collective-permute-start(bf16[512,1024]{1,0:T(8,128)(2,1)} %collective-permute-done.25.rest_16_.rest_20_), channel_id=1, source_target_pairs={{0,2},{2,0},{4,6},{6,4},{8,10},{10,8},{12,14},{14,12},{1,3},{3,1},... | collective-permute-start | bytes 3145736 | tf_op jit(solution)/shard_map/ppermute | solution.py:38
  194.2 29.2 %collective-permute-start.29 = (bf16[512,1024]{1,0:T(8,128)(2,1)}, bf16[512,1024]{1,0:T(8,128)(2,1)}, u32[]{:S(2)}, u32[]{:S(2)}) collective-permute-start(bf16[512,1024]{1,0:T(8,128)(2,1)} %collective-permute-done.25.rest_16_.rest_20_), channel_id=1, source_target_pairs={{0,12},{2,14},{4,0},{6,2},{8,4},{10,6},{12,8},{14,10},{1,13},{3,15... | collective-permute-start | bytes 3145736 | tf_op jit(solution)/shard_map/ppermute | solution.py:34
  197.0 26.4 %collective-permute-start.30 = (bf16[512,1024]{1,0:T(8,128)(2,1)}, bf16[512,1024]{1,0:T(8,128)(2,1)}, u32[]{:S(2)}, u32[]{:S(2)}) collective-permute-start(bf16[512,1024]{1,0:T(8,128)(2,1)} %collective-permute-done.27.rest_22_), channel_id=1, source_target_pairs={{0,4},{2,6},{4,8},{6,10},{8,12},{10,14},{12,0},{14,2},{1,5},{3,7},... | collective-permute-start | bytes 3145736 | tf_op jit(solution)/shard_map/ppermute | solution.py:34
  (39 other events, 583.7 us)

commit v3 on v2

--- a/solution.py
+++ b/solution.py
@@ -48,16 +48,12 @@
 
 
 def ring_weights(shard):
-    half = shard.shape[0] // 2
     up, down = shard, shard
     found = [((0, 0), 0, shard)]
     for step in range(1, 4):
         up, down = z_shift(up, 1), z_shift(down, -1)
         found += [((2 * step - 1, step), 0, up), ((2 * step, step), 0, down)]
-    found += [
-        ((7, 4), 0, z_shift(up[:half], 1)),
-        ((7, 4), half, z_shift(down[half:], -1)),
-    ]
+    found.append(((7, 4), 0, z_shift(up, 1)))
     shards = []
     for (place, step), first, value in found:
         shards.append(((place, 0, first), value))
@@ -280,6 +276,7 @@
     smem = pl.BlockSpec(memory_space=pltpu.SMEM)
     vmem = pl.BlockSpec(memory_space=pltpu.VMEM)
     anyspace = pl.BlockSpec(memory_space=pl.ANY)
+    hbm = pl.BlockSpec(memory_space=pltpu.HBM)
     extra = [] if earlier is None else [earlier]
     return pl.pallas_call(
         functools.partial(attend_kernel, seq=seq, has_in=earlier is not None),
@@ -287,7 +284,7 @@
             jax.ShapeDtypeStruct((slots, seq, GROUP * HD), jnp.bfloat16),
             jax.ShapeDtypeStruct((slots, HD), jnp.float32),
         ),
-        in_specs=[smem, smem, anyspace, anyspace, vmem] + [anyspace] * len(extra),
+        in_specs=[smem, smem, anyspace, hbm, vmem] + [anyspace] * len(extra),
         out_specs=(anyspace, vmem),
         scratch_shapes=[
             pltpu.VMEM(rows.shape, jnp.bfloat16),
@@ -396,6 +393,7 @@
 
     sooner = (ring < 7)[:, None]
     a_soon, b_soon = (0, 1, 2, 3, 5, 6), (0, 1, 2, 3)
+    b_next, b_rest = (0, 1, 2, 3, 4, 5), (6, 7)
     whole = tuple(range(8))
     in_a = jnp.array([p in a_soon for p in whole])[None, :]
     in_b = jnp.array([p in b_soon for p in whole])[None, :]
@@ -404,7 +402,8 @@
             table_row(a_soon, sooner),
             table_row(whole, ~(sooner & in_a)),
             table_row(b_soon, sooner),
-            table_row(whole, ~(sooner & in_b)),
+            table_row(b_next, ~(sooner & in_b)),
+            table_row(b_rest, ring[:, None] >= 0),
         ]
     )
     gain = norm_gain[0].reshape(-1, feats)
@@ -422,7 +421,10 @@
         table, 2, sums_b, gain, weights, [all_b[p] for p in b_soon], hops=7, last=False
     )
     out_a = project(table, 1, sums_a, gain, weights, all_a, acc=part_a)
-    out_b = project(table, 3, sums_b, gain, weights, all_b, acc=part_b)
+    part_b = project(
+        table, 3, sums_b, gain, weights, [all_b[p] for p in b_next], acc=part_b, last=False
+    )
+    out_b = project(table, 4, sums_b, gain, weights, [all_b[p] for p in b_rest], acc=part_b)
 
     out_a = lax.all_to_all(out_a.reshape(peers, seq, -1), "dp", 0, 0, tiled=True)
     out_b = out_b.reshape(peers, seq, -1)

time: 262 us -> 253 us (0.966)
  blocking collectives: 46.2 us -> 9.72 us
  waiting for transfers between devices: 65.6 us -> 91.8 us
  local copies, waits for them, and re-layouts: 21 us -> 12.1 us
  Pallas kernels: 47.5 us -> 52.1 us
    all_to_all x2 -> x1, blocking collectives: 46.2 us -> 9.72 us  [sent_to_all(): lax.all_to_all(jnp.broadcast_to(value[None], (length, *value.shape)), axi...]
    all_to_all x0 -> x1, waiting for transfers between devices: none -> 23.6 us  [sent_to_all(): lax.all_to_all(jnp.broadcast_to(value[None], (length, *value.shape)), axi...]
    ppermute x10, waiting for transfers between devices: 18 us -> 35.8 us  [y_shift(): return lax.ppermute(value, 'tensor', pairs)]
    unnamed x62 -> x44, local copies, waits for them, and re-layouts: 11.5 us -> 2.92 us
    ppermute x8 -> x7, waiting for transfers between devices: 26.7 us -> 19.1 us  [z_shift(): return lax.ppermute(value, 'dp', pairs)]
    ppermute x4, waiting for transfers between devices: 20.5 us -> 13.4 us  [x_swap(): return lax.ppermute(value, 'tensor', [(t, t ^ 1) for t in range(8)])]
    all_to_all x0 -> x1, starting transfers between devices: none -> 5.43 us  [sent_to_all(): lax.all_to_all(jnp.broadcast_to(value[None], (length, *value.shape)), axi...]
    pallas_call x4 -> x5, Pallas kernels: 34.9 us -> 39.5 us  [project(): pl.pallas_call(functools.partial(mm_kernel, row=row, count=count, shards=...]
  transfers between devices with their start and end apart: 33 -> 32, of which waited for: 11 -> 11; matrix products, arithmetic and copies ran while one was open for 7% -> 8% of each run, Pallas kernels for 16% -> 18%
where the time goes in v3:
time: 253 us; the launch traced here: 249 us
  waiting for transfers between devices  91.8 us (36%)
  starting transfers between devices  72.3 us (29%)
  Pallas kernels  52.1 us (21%)
  local copies, waits for them, and re-layouts  12.1 us (5%)
  other arithmetic  9.89 us (4%)
  blocking collectives  9.72 us (4%)
    pallas_call x5, Pallas kernels, project(): pl.pallas_call(functools.partial(mm_kernel, row=row, count=count, shards=...  39.5 us
    ppermute x10, waiting for transfers between devices, y_shift(): return lax.ppermute(value, 'tensor', pairs)  35.8 us
    all_to_all x1, waiting for transfers between devices, sent_to_all(): lax.all_to_all(jnp.broadcast_to(value[None], (length, *value.shape)), axi...  23.6 us
    ppermute x7, waiting for transfers between devices, z_shift(): return lax.ppermute(value, 'dp', pairs)  19.1 us
    ppermute x8, starting transfers between devices, core_swap(): return lax.ppermute(value, 'dp', [(d, d ^ 1) for d in range(16)])  17.2 us
    ppermute x4, waiting for transfers between devices, x_swap(): return lax.ppermute(value, 'tensor', [(t, t ^ 1) for t in range(8)])  13.4 us
    ppermute x7, starting transfers between devices, z_shift(): return lax.ppermute(value, 'dp', pairs)  12.9 us
    ppermute x10, starting transfers between devices, y_shift(): return lax.ppermute(value, 'tensor', pairs)  12.7 us
  transfers between devices with their start and end apart: 32, of which 11 were waited for; matrix products, arithmetic and copies ran while one was open for 8% of the time, Pallas kernels for 18%

profile of v3, /device:TPU:1, one launch (start us, length us, event | category | flops | bytes accessed | tf_op | source)
XLA Modules:
  0.0 249.2 jit_solution(750890865223234399)
XLA Ops:
  3.2 4.0 %collective-permute-start.3 = (bf16[512,768]{1,0:T(8,128)(2,1)}, bf16[512,768]{1,0:T(8,128)(2,1)}, u32[]{:S(2)}, u32[]{:S(2)}) collective-permute-start(bf16[512,768]{1,0:T(8,128)(2,1)} %bitcast.73), channel_id=1, source_target_pairs={{0,224},{16,240},{32,0},{48,16},{64,32},{80,48},{96,64},{112,80},{... | collective-permute-start | bytes 2359304 | tf_op jit(solution)/shard_map/ppermute | solution.py:43
  16.7 6.5 %all-to-all-start = ((bf16[16,32,1024]{2,1,0:T(8,128)(2,1)}), bf16[16,32,1024]{2,1,0:T(8,128)(2,1)}, u32[]{:S(2)}, u32[]{:S(2)}) async-start(bf16[16,32,1024]{2,1,0:T(8,128)(2,1)} %gather_fusion.1), calls=%async_computation | async-start | bytes 2097152 | tf_op jit(solution)/shard_map/all_to_all | solution.py:335
  31.4 6.1 %collective-permute-done.17.rest_17_.rest_19_ = bf16[512,1024]{1,0:T(8,128)(2,1)} collective-permute-done((bf16[512,1024]{1,0:T(8,128)(2,1)}, bf16[512,1024]{1,0:T(8,128)(2,1)}, u32[]{:S(2)}, u32[]{:S(2)}) %collective-permute-start.17) | collective-permute-done | bytes 1048608 | tf_op jit(solution)/shard_map/ppermute | solution.py:38
  41.3 9.4 %collective-permute-done.16.rest_16_.rest_18_ = bf16[512,1024]{1,0:T(8,128)(2,1)} collective-permute-done((bf16[512,1024]{1,0:T(8,128)(2,1)}, bf16[512,1024]{1,0:T(8,128)(2,1)}, u32[]{:S(2)}, u32[]{:S(2)}) %collective-permute-start.16) | collective-permute-done | bytes 1048608 | tf_op jit(solution)/shard_map/ppermute | solution.py:34
  52.0 14.0 %collective-permute-done.5.rest_6_ = bf16[512,768]{1,0:T(8,128)(2,1)} collective-permute-done((bf16[512,768]{1,0:T(8,128)(2,1)}, bf16[512,768]{1,0:T(8,128)(2,1)}, u32[]{:S(2)}, u32[]{:S(2)}) %collective-permute-start.5) | collective-permute-done | bytes 786464 | tf_op jit(solution)/shard_map/ppermute | solution.py:43
  74.5 6.3 %collective-permute-start.6 = (bf16[512,768]{1,0:T(8,128)(2,1)}, bf16[512,768]{1,0:T(8,128)(2,1)}, u32[]{:S(2)}, u32[]{:S(2)}) collective-permute-start(bf16[512,768]{1,0:T(8,128)(2,1)} %collective-permute-done.5.rest_6_), channel_id=1, source_target_pairs={{0,16},{16,0},{32,48},{48,32},{64,80},{80,64},{96,112},{112,96},{1... | collective-permute-start | bytes 2359304 | tf_op jit(solution)/shard_map/ppermute | solution.py:47
  80.9 15.9 %collective-permute-done.18.rest_20_ = bf16[512,1024]{1,0:T(8,128)(2,1)} collective-permute-done((bf16[512,1024]{1,0:T(8,128)(2,1)}, bf16[512,1024]{1,0:T(8,128)(2,1)}, u32[]{:S(2)}, u32[]{:S(2)}) %collective-permute-start.18) | collective-permute-done | bytes 1048608 | tf_op jit(solution)/shard_map/ppermute | solution.py:34
  96.8 6.5 %collective-permute-start.8 = (bf16[512,768]{1,0:T(8,128)(2,1)}, bf16[512,768]{1,0:T(8,128)(2,1)}, u32[]{:S(2)}, u32[]{:S(2)}) collective-permute-start(bf16[512,768]{1,0:T(8,128)(2,1)} %collective-permute-done.7.rest_8_), channel_id=1, source_target_pairs={{0,16},{16,0},{32,48},{48,32},{64,80},{80,64},{96,112},{112,96},{1... | collective-permute-start | bytes 2359304 | tf_op jit(solution)/shard_map/ppermute | solution.py:47
  113.3 6.0 %collective-permute-done.24.rest_15_.rest_17_ = bf16[512,1024]{1,0:T(8,128)(2,1)} collective-permute-done((bf16[512,1024]{1,0:T(8,128)(2,1)}, bf16[512,1024]{1,0:T(8,128)(2,1)}, u32[]{:S(2)}, u32[]{:S(2)}) %collective-permute-start.24) | collective-permute-done | bytes 1048608 | tf_op jit(solution)/shard_map/ppermute | solution.py:34
  119.3 5.0 %collective-permute-done.13.rest_14_ = bf16[512,768]{1,0:T(8,128)(2,1)} collective-permute-done((bf16[512,768]{1,0:T(8,128)(2,1)}, bf16[512,768]{1,0:T(8,128)(2,1)}, u32[]{:S(2)}, u32[]{:S(2)}) %collective-permute-start.13) | collective-permute-done | bytes 786464 | tf_op jit(solution)/shard_map/ppermute | solution.py:43
  127.4 5.4 %all-to-all-start.1 = ((f32[8,1,1024]{2,1,0:T(1,128)}), f32[8,1,1024]{2,1,0:T(1,128)S(1)}, u32[]{:S(2)}, u32[]{:S(2)}) async-start(f32[8,1,1024]{2,1,0:T(1,128)} %broadcast_in_dim.233), calls=%async_computation.1 | async-start | bytes 65536 | tf_op jit(solution)/shard_map/all_to_all | solution.py:27
  135.8 23.6 %all-to-all-done.1 = f32[8,1,1024]{2,1,0:T(1,128)S(1)} async-done(((f32[8,1,1024]{2,1,0:T(1,128)}), f32[8,1,1024]{2,1,0:T(1,128)S(1)}, u32[]{:S(2)}, u32[]{:S(2)}) %all-to-all-start.1) | async-done | bytes 32800 | tf_op jit(solution)/shard_map/all_to_all | solution.py:27
  159.4 4.2 %collective-permute-start.27 = (bf16[512,1024]{1,0:T(8,128)(2,1)}, bf16[512,1024]{1,0:T(8,128)(2,1)}, u32[]{:S(2)}, u32[]{:S(2)}) collective-permute-start(bf16[512,1024]{1,0:T(8,128)(2,1)} %bitcast.37.rest_14_.rest_16_), channel_id=1, source_target_pairs={{0,2},{2,0},{4,6},{6,4},{8,10},{10,8},{12,14},{14,12},{1,3},{3,1},... | collective-permute-start | bytes 3145736 | tf_op jit(solution)/shard_map/ppermute | solution.py:38
  163.6 9.8 %project.5.rest_24_ = f32[512,768]{1,0:T(8,128)} custom-call(s32[5,35]{1,0:T(8,128)S(1)} %stack.45.table_ref, f32[8,512]{1,0:T(8,128)S(1)} %get-tuple-element.37.sums_ref, f32[8,1024]{1,0:T(8,128)S(1)} %reshape_squeeze.7.gain_ref, bf16[512,768]{1,0:T(8,128)(2,1)S(1)} %bitcast.75, bf16[512,768]{1,0:T(8,128)(2,1)} %collective-permute-done.rest_1_, ...), custom_call_target="tpu_custom_call" | custom-call | flops 3221225472 | bytes 10485760 | tf_op jit(solution)/shard_map/project/pallas_call | solution.py:147
  174.9 7.9 %project.6 = bf16[512,768]{1,0:T(8,128)(2,1)S(1)} custom-call(s32[5,35]{1,0:T(8,128)S(1)} %stack.45.table_ref, f32[8,512]{1,0:T(8,128)S(1)} %get-tuple-element.37.sums_ref, f32[8,1024]{1,0:T(8,128)S(1)} %reshape_squeeze.7.gain_ref, bf16[512,768]{1,0:T(8,128)(2,1)S(1)} %bitcast.76, bf16[512,768]{1,0:T(8,128)(2,1)} %collective-permute-done.rest_1_, ...), custom_call_target="tpu_custom_call" | custom-call | flops 3221225472 | bytes 10485760 | tf_op jit(solution)/shard_map/project/pallas_call | solution.py:147
  183.7 6.3 %all-to-all-start.2 = ((bf16[16,32,768]{2,1,0:T(8,128)(2,1)}), bf16[16,32,768]{2,1,0:T(8,128)(2,1)}, u32[]{:S(2)}, u32[]{:S(2)}) async-start(bf16[16,32,768]{2,1,0:T(8,128)(2,1)} %bitcast.80), calls=%async_computation.2 | async-start | bytes 1572864 | tf_op jit(solution)/shard_map/all_to_all | solution.py:429
  190.0 3.0 %collective-permute-start.23 = (bf16[512,1024]{1,0:T(8,128)(2,1)}, bf16[512,1024]{1,0:T(8,128)(2,1)}, u32[]{:S(2)}, u32[]{:S(2)}) collective-permute-start(bf16[512,1024]{1,0:T(8,128)(2,1)} %collective-permute-done.22.rest_16_.rest_18_), channel_id=1, source_target_pairs={{0,12},{2,14},{4,0},{6,2},{8,4},{10,6},{12,8},{14,10},{1,13},{3,15... | collective-permute-start | bytes 3145736 | tf_op jit(solution)/shard_map/ppermute | solution.py:34
  193.0 8.5 %project.7.rest_22_ = f32[512,768]{1,0:T(8,128)} custom-call(s32[5,35]{1,0:T(8,128)S(1)} %stack.45.table_ref, f32[8,512]{1,0:T(8,128)S(1)} %get-tuple-element.36.sums_ref, f32[8,1024]{1,0:T(8,128)S(1)} %reshape_squeeze.7.gain_ref, bf16[512,768]{1,0:T(8,128)(2,1)S(1)} %bitcast.77, bf16[512,768]{1,0:T(8,128)(2,1)} %collective-permute-done.rest_1_, ...), custom_call_target="tpu_custom_call" | custom-call | flops 3221225472 | bytes 10485760 | tf_op jit(solution)/shard_map/project/pallas_call | solution.py:147
  201.5 7.2 %collective-permute-done.28.rest_21_ = bf16[512,1024]{1,0:T(8,128)(2,1)} collective-permute-done((bf16[512,1024]{1,0:T(8,128)(2,1)}, bf16[512,1024]{1,0:T(8,128)(2,1)}, u32[]{:S(2)}, u32[]{:S(2)}) %collective-permute-start.28) | collective-permute-done | bytes 1048608 | tf_op jit(solution)/shard_map/ppermute | solution.py:38
  208.8 7.2 %project.8.rest_18_ = f32[512,768]{1,0:T(8,128)} custom-call(s32[5,35]{1,0:T(8,128)S(1)} %stack.45.table_ref, f32[8,512]{1,0:T(8,128)S(1)} %get-tuple-element.36.sums_ref, f32[8,1024]{1,0:T(8,128)S(1)} %reshape_squeeze.7.gain_ref, bf16[512,768]{1,0:T(8,128)(2,1)S(1)} %bitcast.78, bf16[512,768]{1,0:T(8,128)(2,1)} %collective-permute-done.rest_1_, ...), custom_call_target="tpu_custom_call" | custom-call | flops 3221225472 | bytes 10485760 | tf_op jit(solution)/shard_map/project/pallas_call | solution.py:147
  218.5 6.0 %project.9 = bf16[512,768]{1,0:T(8,128)(2,1)S(1)} custom-call(s32[5,35]{1,0:T(8,128)S(1)} %stack.45.table_ref, f32[8,512]{1,0:T(8,128)S(1)} %get-tuple-element.36.sums_ref, f32[8,1024]{1,0:T(8,128)S(1)} %reshape_squeeze.7.gain_ref, bf16[512,768]{1,0:T(8,128)(2,1)S(1)} %bitcast.79, bf16[512,768]{1,0:T(8,128)(2,1)} %collective-permute-done.rest_1_, ...), custom_call_target="tpu_custom_call" | custom-call | flops 1610612736 | bytes 5242880 | tf_op jit(solution)/shard_map/project/pallas_call | solution.py:147
  224.6 6.4 %attend.2 = (bf16[32,32,512]{2,1,0:T(8,128)(2,1)}, f32[32,128]{1,0:T(8,128)S(1)}) custom-call(s32[3,16]{1,0:T(4,128)S(1)} %get-tuple-element.15.meta_ref, s32[4]{0:T(128)S(1)} %copy-done.6, bf16[16,32,768]{2,1,0:T(8,128)(2,1)S(1)} %bitcast.83, bf16[4,768,256]{2,1,0:T(8,128)(2,1)S(1)} %bitcast.81, f32[4,128]{1,0:T(4,128)S(1)} %bitcast.84), custom_call_target="tpu_custom_call" | custom-call | flops 805306368 | bytes 3407872 | tf_op jit(solution)/shard_map/attend/pallas_call | solution.py:281
  232.3 6.3 %attend.3 = (bf16[32,32,512]{2,1,0:T(8,128)(2,1)}, f32[32,128]{1,0:T(8,128)S(1)}) custom-call(s32[3,16]{1,0:T(4,128)S(1)} %get-tuple-element.11.meta_ref, s32[4]{0:T(128)S(1)} %copy-done.6, bf16[16,32,768]{2,1,0:T(8,128)(2,1)} %all-to-all-done.2.rows_hbm, bf16[4,768,256]{2,1,0:T(8,128)(2,1)S(1)} %bitcast.82, ...), custom_call_target="tpu_custom_call", output_to_operand_aliasing={{0}: (5, {})} | custom-call | flops 805306368 | bytes 3407872 | tf_op jit(solution)/shard_map/attend/pallas_call | solution.py:281
  238.8 9.7 %all_to_all.24 = f32[16,4,8]{2,1,0:T(4,128)S(1)} all-to-all(f32[16,4,8]{2,1,0:T(4,128)S(1)} %broadcast_in_dim.234), channel_id=1, replica_groups=mesh['dp'=16,'tensor'=8,'mp'=2] {'tensor','mp'}, dimensions={0} | all-to-all | bytes 4096 | tf_op jit(solution)/shard_map/all_to_all | solution.py:27
  (175 shorter events, 56.7 us)
Async XLA Ops:
  11.0 26.5 %collective-permute-start.17 = (bf16[512,1024]{1,0:T(8,128)(2,1)}, bf16[512,1024]{1,0:T(8,128)(2,1)}, u32[]{:S(2)}, u32[]{:S(2)}) collective-permute-start(bf16[512,1024]{1,0:T(8,128)(2,1)} %bitcast.86), channel_id=1, source_target_pairs={{0,2},{2,0},{4,6},{6,4},{8,10},{10,8},{12,14},{14,12},{1,3},{3,1},... | collective-permute-start | bytes 3145736 | tf_op jit(solution)/shard_map/ppermute | solution.py:38
  13.7 26.1 %collective-permute-start.15 = (bf16[512,1024]{1,0:T(8,128)(2,1)}, bf16[512,1024]{1,0:T(8,128)(2,1)}, u32[]{:S(2)}, u32[]{:S(2)}) collective-permute-start(bf16[512,1024]{1,0:T(8,128)(2,1)} %bitcast.87), channel_id=1, source_target_pairs={{0,4},{2,6},{4,8},{6,10},{8,12},{10,14},{12,0},{14,2},{1,5},{3,7},... | collective-permute-start | bytes 3145736 | tf_op jit(solution)/shard_map/ppermute | solution.py:34
  16.7 55.7 %all-to-all-start = ((bf16[16,32,1024]{2,1,0:T(8,128)(2,1)}), bf16[16,32,1024]{2,1,0:T(8,128)(2,1)}, u32[]{:S(2)}, u32[]{:S(2)}) async-start(bf16[16,32,1024]{2,1,0:T(8,128)(2,1)} %gather_fusion.1), calls=%async_computation | async-start | bytes 2097152 | tf_op jit(solution)/shard_map/all_to_all | solution.py:335
  27.8 38.3 %collective-permute-start.5 = (bf16[512,768]{1,0:T(8,128)(2,1)}, bf16[512,768]{1,0:T(8,128)(2,1)}, u32[]{:S(2)}, u32[]{:S(2)}) collective-permute-start(bf16[512,768]{1,0:T(8,128)(2,1)} %collective-permute-done.1.rest_2_), channel_id=1, source_target_pairs={{0,32},{16,48},{32,64},{48,80},{64,96},{80,112},{96,128},{112,144}... | collective-permute-start | bytes 2359304 | tf_op jit(solution)/shard_map/ppermute | solution.py:43
  28.9 38.1 %collective-permute-start.7 = (bf16[512,768]{1,0:T(8,128)(2,1)}, bf16[512,768]{1,0:T(8,128)(2,1)}, u32[]{:S(2)}, u32[]{:S(2)}) collective-permute-start(bf16[512,768]{1,0:T(8,128)(2,1)} %collective-permute-done.3.rest_4_), channel_id=1, source_target_pairs={{0,224},{16,240},{32,0},{48,16},{64,32},{80,48},{96,64},{112,80},{... | collective-permute-start | bytes 2359304 | tf_op jit(solution)/shard_map/ppermute | solution.py:43
  37.5 31.9 %collective-permute-start.2 = (bf16[512,768]{1,0:T(8,128)(2,1)}, bf16[512,768]{1,0:T(8,128)(2,1)}, u32[]{:S(2)}, u32[]{:S(2)}) collective-permute-start(bf16[512,768]{1,0:T(8,128)(2,1)} %collective-permute-done.1.rest_2_), channel_id=1, source_target_pairs={{0,16},{16,0},{32,48},{48,32},{64,80},{80,64},{96,112},{112,96},{1... | collective-permute-start | bytes 2359304 | tf_op jit(solution)/shard_map/ppermute | solution.py:47
  39.9 33.3 %collective-permute-start.19 = (bf16[512,1024]{1,0:T(8,128)(2,1)}, bf16[512,1024]{1,0:T(8,128)(2,1)}, u32[]{:S(2)}, u32[]{:S(2)}) collective-permute-start(bf16[512,1024]{1,0:T(8,128)(2,1)} %collective-permute-done.17.rest_17_.rest_19_), channel_id=1, source_target_pairs={{0,12},{2,14},{4,0},{6,2},{8,4},{10,6},{12,8},{14,10},{1,13},{3,15... | collective-permute-start | bytes 3145736 | tf_op jit(solution)/shard_map/ppermute | solution.py:34
  67.1 29.7 %collective-permute-start.18 = (bf16[512,1024]{1,0:T(8,128)(2,1)}, bf16[512,1024]{1,0:T(8,128)(2,1)}, u32[]{:S(2)}, u32[]{:S(2)}) collective-permute-start(bf16[512,1024]{1,0:T(8,128)(2,1)} %collective-permute-done.17.rest_17_.rest_19_), channel_id=1, source_target_pairs={{0,4},{2,6},{4,8},{6,10},{8,12},{10,14},{12,0},{14,2},{1,5},{3,7},... | collective-permute-start | bytes 3145736 | tf_op jit(solution)/shard_map/ppermute | solution.py:34
  69.4 34.2 %collective-permute-start.9 = (bf16[512,768]{1,0:T(8,128)(2,1)}, bf16[512,768]{1,0:T(8,128)(2,1)}, u32[]{:S(2)}, u32[]{:S(2)}) collective-permute-start(bf16[512,768]{1,0:T(8,128)(2,1)} %collective-permute-done.5.rest_6_), channel_id=1, source_target_pairs={{0,32},{16,48},{32,64},{48,80},{64,96},{80,112},{96,128},{112,144}... | collective-permute-start | bytes 2359304 | tf_op jit(solution)/shard_map/ppermute | solution.py:43
  69.5 35.0 %collective-permute-start.11 = (bf16[512,768]{1,0:T(8,128)(2,1)}, bf16[512,768]{1,0:T(8,128)(2,1)}, u32[]{:S(2)}, u32[]{:S(2)}) collective-permute-start(bf16[512,768]{1,0:T(8,128)(2,1)} %collective-permute-done.7.rest_8_), channel_id=1, source_target_pairs={{0,224},{16,240},{32,0},{48,16},{64,32},{80,48},{96,64},{112,80},{... | collective-permute-start | bytes 2359304 | tf_op jit(solution)/shard_map/ppermute | solution.py:43
  73.1 46.1 %collective-permute-start.24 = (bf16[512,1024]{1,0:T(8,128)(2,1)}, bf16[512,1024]{1,0:T(8,128)(2,1)}, u32[]{:S(2)}, u32[]{:S(2)}) collective-permute-start(bf16[512,1024]{1,0:T(8,128)(2,1)} %bitcast.37.rest_14_.rest_16_), channel_id=1, source_target_pairs={{0,4},{2,6},{4,8},{6,10},{8,12},{10,14},{12,0},{14,2},{1,5},{3,7},... | collective-permute-start | bytes 3145736 | tf_op jit(solution)/shard_map/ppermute | solution.py:34
  74.5 31.9 %collective-permute-start.6 = (bf16[512,768]{1,0:T(8,128)(2,1)}, bf16[512,768]{1,0:T(8,128)(2,1)}, u32[]{:S(2)}, u32[]{:S(2)}) collective-permute-start(bf16[512,768]{1,0:T(8,128)(2,1)} %collective-permute-done.5.rest_6_), channel_id=1, source_target_pairs={{0,16},{16,0},{32,48},{48,32},{64,80},{80,64},{96,112},{112,96},{1... | collective-permute-start | bytes 2359304 | tf_op jit(solution)/shard_map/ppermute | solution.py:47
  104.5 28.3 %collective-permute-start.10 = (bf16[512,768]{1,0:T(8,128)(2,1)}, bf16[512,768]{1,0:T(8,128)(2,1)}, u32[]{:S(2)}, u32[]{:S(2)}) collective-permute-start(bf16[512,768]{1,0:T(8,128)(2,1)} %collective-permute-done.9.rest_10_), channel_id=1, source_target_pairs={{0,16},{16,0},{32,48},{48,32},{64,80},{80,64},{96,112},{112,96},{1... | collective-permute-start | bytes 2359304 | tf_op jit(solution)/shard_map/ppermute | solution.py:47
  106.4 53.0 %collective-permute-start.12 = (bf16[512,768]{1,0:T(8,128)(2,1)}, bf16[512,768]{1,0:T(8,128)(2,1)}, u32[]{:S(2)}, u32[]{:S(2)}) collective-permute-start(bf16[512,768]{1,0:T(8,128)(2,1)} %collective-permute-done.11.rest_12_), channel_id=1, source_target_pairs={{0,16},{16,0},{32,48},{48,32},{64,80},{80,64},{96,112},{112,96},{1... | collective-permute-start | bytes 2359304 | tf_op jit(solution)/shard_map/ppermute | solution.py:47
  111.8 61.6 %collective-permute-start.22 = (bf16[512,1024]{1,0:T(8,128)(2,1)}, bf16[512,1024]{1,0:T(8,128)(2,1)}, u32[]{:S(2)}, u32[]{:S(2)}) collective-permute-start(bf16[512,1024]{1,0:T(8,128)(2,1)} %bitcast.37.rest_14_.rest_16_), channel_id=1, source_target_pairs={{0,12},{2,14},{4,0},{6,2},{8,4},{10,6},{12,8},{14,10},{1,13},{3,15... | collective-permute-start | bytes 3145736 | tf_op jit(solution)/shard_map/ppermute | solution.py:34
  119.2 55.6 %collective-permute-start.21 = (bf16[512,1024]{1,0:T(8,128)(2,1)}, bf16[512,1024]{1,0:T(8,128)(2,1)}, u32[]{:S(2)}, u32[]{:S(2)}) collective-permute-start(bf16[512,1024]{1,0:T(8,128)(2,1)} %collective-permute-done.19.rest_18_.rest_21_), channel_id=1, source_target_pairs={{0,12},{2,14},{4,0},{6,2},{8,4},{10,6},{12,8},{14,10},{1,13},{3,15... | collective-permute-start | bytes 3145736 | tf_op jit(solution)/shard_map/ppermute | solution.py:34
  124.3 50.5 %collective-permute-start.14 = (bf16[512,768]{1,0:T(8,128)(2,1)}, bf16[512,768]{1,0:T(8,128)(2,1)}, u32[]{:S(2)}, u32[]{:S(2)}) collective-permute-start(bf16[512,768]{1,0:T(8,128)(2,1)} %collective-permute-done.13.rest_14_), channel_id=1, source_target_pairs={{0,16},{16,0},{32,48},{48,32},{64,80},{80,64},{96,112},{112,96},{1... | collective-permute-start | bytes 2359304 | tf_op jit(solution)/shard_map/ppermute | solution.py:47
  127.4 32.0 %all-to-all-start.1 = ((f32[8,1,1024]{2,1,0:T(1,128)}), f32[8,1,1024]{2,1,0:T(1,128)S(1)}, u32[]{:S(2)}, u32[]{:S(2)}) async-start(f32[8,1,1024]{2,1,0:T(1,128)} %broadcast_in_dim.233), calls=%async_computation.1 | async-start | bytes 65536 | tf_op jit(solution)/shard_map/all_to_all | solution.py:27
  132.9 60.1 %collective-permute-start.25 = (bf16[512,1024]{1,0:T(8,128)(2,1)}, bf16[512,1024]{1,0:T(8,128)(2,1)}, u32[]{:S(2)}, u32[]{:S(2)}) collective-permute-start(bf16[512,1024]{1,0:T(8,128)(2,1)} %collective-permute-done.24.rest_15_.rest_17_), channel_id=1, source_target_pairs={{0,2},{2,0},{4,6},{6,4},{8,10},{10,8},{12,14},{14,12},{1,3},{3,1},... | collective-permute-start | bytes 3145736 | tf_op jit(solution)/shard_map/ppermute | solution.py:38
  159.4 33.6 %collective-permute-start.27 = (bf16[512,1024]{1,0:T(8,128)(2,1)}, bf16[512,1024]{1,0:T(8,128)(2,1)}, u32[]{:S(2)}, u32[]{:S(2)}) collective-permute-start(bf16[512,1024]{1,0:T(8,128)(2,1)} %bitcast.37.rest_14_.rest_16_), channel_id=1, source_target_pairs={{0,2},{2,0},{4,6},{6,4},{8,10},{10,8},{12,14},{14,12},{1,3},{3,1},... | collective-permute-start | bytes 3145736 | tf_op jit(solution)/shard_map/ppermute | solution.py:38
  173.4 35.3 %collective-permute-start.28 = (bf16[512,1024]{1,0:T(8,128)(2,1)}, bf16[512,1024]{1,0:T(8,128)(2,1)}, u32[]{:S(2)}, u32[]{:S(2)}) collective-permute-start(bf16[512,1024]{1,0:T(8,128)(2,1)} %collective-permute-done.22.rest_16_.rest_18_), channel_id=1, source_target_pairs={{0,2},{2,0},{4,6},{6,4},{8,10},{10,8},{12,14},{14,12},{1,3},{3,1},... | collective-permute-start | bytes 3145736 | tf_op jit(solution)/shard_map/ppermute | solution.py:38
  183.7 47.3 %all-to-all-start.2 = ((bf16[16,32,768]{2,1,0:T(8,128)(2,1)}), bf16[16,32,768]{2,1,0:T(8,128)(2,1)}, u32[]{:S(2)}, u32[]{:S(2)}) async-start(bf16[16,32,768]{2,1,0:T(8,128)(2,1)} %bitcast.80), calls=%async_computation.2 | async-start | bytes 1572864 | tf_op jit(solution)/shard_map/all_to_all | solution.py:429
  190.0 26.1 %collective-permute-start.23 = (bf16[512,1024]{1,0:T(8,128)(2,1)}, bf16[512,1024]{1,0:T(8,128)(2,1)}, u32[]{:S(2)}, u32[]{:S(2)}) collective-permute-start(bf16[512,1024]{1,0:T(8,128)(2,1)} %collective-permute-done.22.rest_16_.rest_18_), channel_id=1, source_target_pairs={{0,12},{2,14},{4,0},{6,2},{8,4},{10,6},{12,8},{14,10},{1,13},{3,15... | collective-permute-start | bytes 3145736 | tf_op jit(solution)/shard_map/ppermute | solution.py:34
  193.0 25.5 %collective-permute-start.26 = (bf16[512,1024]{1,0:T(8,128)(2,1)}, bf16[512,1024]{1,0:T(8,128)(2,1)}, u32[]{:S(2)}, u32[]{:S(2)}) collective-permute-start(bf16[512,1024]{1,0:T(8,128)(2,1)} %collective-permute-done.25.rest_20_), channel_id=1, source_target_pairs={{0,4},{2,6},{4,8},{6,10},{8,12},{10,14},{12,0},{14,2},{1,5},{3,7},... | collective-permute-start | bytes 3145736 | tf_op jit(solution)/shard_map/ppermute | solution.py:34
  (29 other events, 543.7 us)

commit v4 on v3

--- a/solution.py
+++ b/solution.py
@@ -61,13 +61,123 @@
     return shards
 
 
+def add_pieces(
+    table_ref, row, gain_ref, first, before, xbuf, wbuf, acc, inverse, high, low, xsem, wsem
+):
+    part = acc.shape[0] // 2
+    used = table_ref[row, 34]
+    upper, lower = pl.ds(0, part), pl.ds(part, part)
+
+    def ready(i):
+        p = table_ref[row, table_ref[row, 26 + i]] + first
+        pltpu.make_async_copy(xbuf.at[p], xbuf.at[p], xsem.at[p]).wait()
+
+    def normed(i, at):
+        k = table_ref[row, 26 + i]
+        gain = gain_ref[pl.ds(table_ref[row, 8 + k], 1), :]
+        x = xbuf[table_ref[row, k] + first, at, :].astype(jnp.float32)
+        return (x * inverse[at, :] * gain).astype(jnp.bfloat16)
+
+    def visit(i, carry):
+        k = table_ref[row, 26 + i]
+        following = jnp.minimum(i + 1, used - 1)
+        pl.when(i + 1 < used)(lambda: ready(following))
+        arrive = pltpu.make_async_copy(wbuf.at[k], wbuf.at[k], wsem.at[k])
+        if before is None:
+            arrive.wait()
+        else:
+            pl.when(table_ref[before, k] < 0)(arrive.wait)
+        low[...] = normed(i, lower)
+        acc[upper, :] += jnp.dot(high[...], wbuf[k], preferred_element_type=jnp.float32)
+        high[...] = normed(following, upper)
+        acc[lower, :] += jnp.dot(low[...], wbuf[k], preferred_element_type=jnp.float32)
+        return carry
+
+    @pl.when(used > 0)
+    def _():
+        ready(0)
+        high[...] = normed(0, upper)
+        lax.fori_loop(0, used, visit, 0)
+
+
+def soon_kernel(table_ref, sums_a, sums_b, gain_ref, *rest, rows, counts, shards, width):
+    weights, rest = rest[: len(shards)], rest[len(shards) :]
+    pieces, rest = rest[: sum(counts)], rest[sum(counts) :]
+    out_a, out_b, xbuf, wbuf, inverse, high, low, xsem, wsem = rest
+    row_a, row_b = rows
+    for p in range(sum(counts)):
+        row, at = (row_a, p) if p < counts[0] else (row_b, p - counts[0])
+
+        @pl.when(table_ref[row, 18 + at] > 0)
+        def _(p=p):
+            pltpu.make_async_copy(pieces[p], xbuf.at[p], xsem.at[p]).start()
+
+    for k in range(8):
+        mine = [(ref, key) for ref, key in zip(weights, shards) if key[0] == k]
+        if mine:
+
+            @pl.when((table_ref[row_a, k] >= 0) | (table_ref[row_b, k] >= 0))
+            def _(k=k, mine=mine):
+                for ref, (_, other, first) in mine:
+                    start = pl.multiple_of(table_ref[row_a, 16 + other] + first, 256)
+                    pltpu.make_async_copy(
+                        ref, wbuf.at[k, pl.ds(start, ref.shape[0])], wsem.at[k]
+                    ).start()
+
+    parts = ((row_a, 0, None, sums_a, out_a), (row_b, counts[0], row_a, sums_b, out_b))
+    for row, first, before, sums_ref, out in parts:
+        total = jnp.sum(jnp.transpose(sums_ref[...]), axis=1, keepdims=True)
+        inverse[...] = lax.rsqrt(total * (1.0 / width) + norm_eps)
+        out[...] = jnp.zeros_like(out)
+        add_pieces(
+            table_ref, row, gain_ref, first, before, xbuf, wbuf, out, inverse, high, low, xsem, wsem
+        )
+
+
+def project_soon(table, rows, sums, gain, weights, pieces, hops):
+    weights = [pair for pair in weights if pair[0][0] < hops]
+    shards = tuple(key for key, _ in weights)
+    weights = [value for _, value in weights]
+    blocks, feats = gain.shape
+    columns = weights[0].shape[1]
+    height = sums[0].shape[1]
+    counts = tuple(len(part) for part in pieces)
+    smem = pl.BlockSpec(memory_space=pltpu.SMEM)
+    vmem = pl.BlockSpec(memory_space=pltpu.VMEM)
+    anyspace = pl.BlockSpec(memory_space=pl.ANY)
+    shape = jax.ShapeDtypeStruct((height, columns), jnp.float32)
+    return pl.pallas_call(
+        functools.partial(
+            soon_kernel, rows=rows, counts=counts, shards=shards, width=feats * blocks
+        ),
+        out_shape=(shape, shape),
+        in_specs=[smem, vmem, vmem, vmem] + [anyspace] * (len(weights) + sum(counts)),
+        out_specs=(vmem, vmem),
+        scratch_shapes=[
+            pltpu.VMEM((sum(counts), height, feats), jnp.bfloat16),
+            pltpu.VMEM((blocks, feats, columns), jnp.bfloat16),
+            pltpu.VMEM((height, 1), jnp.float32),
+            pltpu.VMEM((height // 2, feats), jnp.bfloat16),
+            pltpu.VMEM((height // 2, feats), jnp.bfloat16),
+            pltpu.SemaphoreType.DMA((sum(counts),)),
+            pltpu.SemaphoreType.DMA((blocks,)),
+        ],
+        compiler_params=pltpu.CompilerParams(vmem_limit_bytes=44 << 20),
+        cost_estimate=pl.CostEstimate(
+            flops=2 * height * columns * feats * 8,
+            bytes_accessed=16 * feats * (height + columns),
+            transcendentals=0,
+        ),
+        name="project_soon",
+    )(table, *sums, gain, *weights, *pieces[0], *pieces[1])
+
+
 def mm_kernel(table_ref, sums_ref, gain_ref, *rest, row, count, shards, has_acc, last, width):
     weights, rest = rest[: len(shards)], rest[len(shards) :]
     pieces, rest = rest[:count], rest[count:]
     if has_acc:
         acc_in, rest = rest[0], rest[1:]
     out_ref, xbuf, wbuf, acc, inverse, high, low, xsem, wsem, asem = rest
-    part = xbuf.shape[1] // 2
     for p in range(count):
 
         @pl.when(table_ref[row, 18 + p] > 0)
@@ -95,36 +205,7 @@
         load.wait()
     else:
         acc[...] = jnp.zeros_like(acc)
-    used = table_ref[row, 34]
-    upper, lower = pl.ds(0, part), pl.ds(part, part)
-
-    def ready(i):
-        p = table_ref[row, table_ref[row, 26 + i]]
-        pltpu.make_async_copy(xbuf.at[p], xbuf.at[p], xsem.at[p]).wait()
-
-    def normed(i, at):
-        k = table_ref[row, 26 + i]
-        gain = gain_ref[pl.ds(table_ref[row, 8 + k], 1), :]
-        x = xbuf[table_ref[row, k], at, :].astype(jnp.float32)
-        return (x * inverse[at, :] * gain).astype(jnp.bfloat16)
-
-    def visit(i, carry):
-        k = table_ref[row, 26 + i]
-        following = jnp.minimum(i + 1, used - 1)
-        pl.when(i + 1 < used)(lambda: ready(following))
-        pltpu.make_async_copy(wbuf.at[k], wbuf.at[k], wsem.at[k]).wait()
-        low[...] = normed(i, lower)
-        acc[upper, :] += jnp.dot(high[...], wbuf[k], preferred_element_type=jnp.float32)
-        high[...] = normed(following, upper)
-        acc[lower, :] += jnp.dot(low[...], wbuf[k], preferred_element_type=jnp.float32)
-        return carry
-
-    @pl.when(used > 0)
-    def _():
-        ready(0)
-        high[...] = normed(0, upper)
-        lax.fori_loop(0, used, visit, 0)
-
+    add_pieces(table_ref, row, gain_ref, 0, None, xbuf, wbuf, acc, inverse, high, low, xsem, wsem)
     if last:
         out_ref[...] = acc[...].astype(out_ref.dtype)
     else:
@@ -190,9 +271,10 @@
     factor = (HD ** (-0.5)) * LOG2E
     token = lax.broadcasted_iota(jnp.int32, (wide, 1), 0) % seq
     column = lax.broadcasted_iota(jnp.int32, (1, positions), 1)
-    causal = lax.broadcasted_iota(jnp.int32, (wide, seq), 1) <= (
-        lax.broadcasted_iota(jnp.int32, (wide, seq), 0) % seq
-    )
+    causal = lax.broadcasted_iota(jnp.int32, (wide, HD), 1) <= (
+        lax.broadcasted_iota(jnp.int32, (wide, HD), 0) % seq
+    )
+    blank = jnp.zeros((HD - seq, HD), jnp.bfloat16)
     value_ref[...] = jnp.zeros_like(value_ref)
     weights = jnp.concatenate(
         [jnp.broadcast_to(score_ref[g : g + 1, :], (seq, HD)) for g in range(GROUP)], axis=0
@@ -214,45 +296,38 @@
         leaf = [meta_ref[0, i] for i in at]
         slot = [meta_ref[1, i] for i in at]
         length = [meta_ref[2, i] for i in at]
-        far, own = [], []
+        scores = []
         for i, one in zip(at, leaf):
             queries = jnp.concatenate(
                 [rows_ref[i, :, g * HD : (g + 1) * HD] for g in range(GROUP)], axis=0
             )
-            key_own = rows_ref[i, :, GROUP * HD : (GROUP + 1) * HD]
-            far.append(
-                lax.dot_general(
-                    queries, cache_ref[one, :, :HD], contract, preferred_element_type=jnp.float32
+            key_own = jnp.concatenate(
+                [rows_ref[i, :, GROUP * HD : (GROUP + 1) * HD], blank], axis=0
+            )
+            far = lax.dot_general(
+                queries, cache_ref[one, :, :HD], contract, preferred_element_type=jnp.float32
+            )
+            own = lax.dot_general(
+                queries, key_own, contract, preferred_element_type=jnp.float32
+            )
+            far = far + jnp.where(column < clen_ref[one], 0.0, -jnp.inf)
+            own = jnp.where(causal, own, -jnp.inf)
+            scores.append(jnp.concatenate([far, own], axis=1))
+        top = [jnp.max(v, axis=1, keepdims=True) for v in scores]
+        probs = [jnp.exp2((v - t) * factor) for v, t in zip(scores, top)]
+        total = [jnp.sum(v, axis=1, keepdims=True) for v in probs]
+        context = []
+        for v, one, i in zip(probs, leaf, at):
+            rounded = v.astype(jnp.bfloat16)
+            value_own = jnp.concatenate([rows_ref[i, :, (GROUP + 1) * HD :], blank], axis=0)
+            context.append(
+                jnp.dot(
+                    rounded[:, :positions],
+                    cache_ref[one, :, HD:],
+                    preferred_element_type=jnp.float32,
                 )
+                + jnp.dot(rounded[:, positions:], value_own, preferred_element_type=jnp.float32)
             )
-            own.append(
-                lax.dot_general(queries, key_own, contract, preferred_element_type=jnp.float32)
-            )
-        far = [
-            f + jnp.where(column < clen_ref[one], 0.0, -jnp.inf) for f, one in zip(far, leaf)
-        ]
-        own = [jnp.where(causal, o, -jnp.inf) for o in own]
-        top = [
-            jnp.maximum(jnp.max(f, axis=1, keepdims=True), jnp.max(o, axis=1, keepdims=True))
-            for f, o in zip(far, own)
-        ]
-        far = [jnp.exp2((f - t) * factor) for f, t in zip(far, top)]
-        own = [jnp.exp2((o - t) * factor) for o, t in zip(own, top)]
-        total = [
-            jnp.sum(f, axis=1, keepdims=True) + jnp.sum(o, axis=1, keepdims=True)
-            for f, o in zip(far, own)
-        ]
-        context = [
-            jnp.dot(
-                f.astype(jnp.bfloat16), cache_ref[one, :, HD:], preferred_element_type=jnp.float32
-            )
-            + jnp.dot(
-                o.astype(jnp.bfloat16),
-                rows_ref[i, :, (GROUP + 1) * HD :],
-                preferred_element_type=jnp.float32,
-            )
-            for f, o, one, i in zip(far, own, leaf, at)
-        ]
         for c, t, i, place, count in zip(context, total, at, slot, length):
             c = jnp.where(token < count, c * (1.0 / t), 0.0)
             for g in range(GROUP):
@@ -414,11 +489,14 @@
     sums_a, sums_b = sums[:, :rows], sums[:, rows:]
     all_a = [a, a_left, a_right, a_x, ax_left, ax_right, a_far, ax_far]
     all_b = [b, b_left, b_right, b_x, bx_left, bx_right, b_far, bx_far]
-    part_a = project(
-        table, 0, sums_a, gain, weights, [all_a[p] for p in a_soon], hops=7, last=False
-    )
-    part_b = project(
-        table, 2, sums_b, gain, weights, [all_b[p] for p in b_soon], hops=7, last=False
+    part_a, part_b = project_soon(
+        table,
+        (0, 2),
+        (sums_a, sums_b),
+        gain,
+        weights,
+        ([all_a[p] for p in a_soon], [all_b[p] for p in b_soon]),
+        hops=7,
     )
     out_a = project(table, 1, sums_a, gain, weights, all_a, acc=part_a)
     part_b = project(

time: 253 us -> 233 us (0.921); the launches traced: 249 us -> 232 us
  waiting for transfers between devices: 91.8 us -> 67.4 us
  blocking collectives: 9.72 us -> 31.9 us
  starting transfers between devices: 72.3 us -> 54.1 us
  local copies, waits for them, and re-layouts: 12.1 us -> 18.6 us
  Pallas kernels: 52.1 us -> 49.1 us
    all_to_all x1 -> x0, waiting for transfers between devices: 23.6 us -> none  [sent_to_all(): lax.all_to_all(jnp.broadcast_to(value[None], (length, *value.shape)), axi...]
    all_to_all x1 -> x2, blocking collectives: 9.72 us -> 31.9 us  [sent_to_all(): lax.all_to_all(jnp.broadcast_to(value[None], (length, *value.shape)), axi...]
    pallas_call x5 -> x3, Pallas kernels: 39.5 us -> 19.5 us  [project(): pl.pallas_call(functools.partial(mm_kernel, row=row, count=count, shards=...]
    pallas_call x0 -> x1, Pallas kernels: none -> 16.9 us  [project_soon(): pl.pallas_call(functools.partial(soon_kernel, rows=rows, counts=counts, s...]
    unnamed x44 -> x62, local copies, waits for them, and re-layouts: 2.92 us -> 10.1 us
    ppermute x8, starting transfers between devices: 17.2 us -> 10.6 us  [core_swap(): return lax.ppermute(value, 'dp', [(d, d ^ 1) for d in range(16)])]
    all_to_all x1 -> x0, starting transfers between devices: 5.43 us -> none  [sent_to_all(): lax.all_to_all(jnp.broadcast_to(value[None], (length, *value.shape)), axi...]
    ppermute x4, starting transfers between devices: 11.3 us -> 5.94 us  [x_swap(): return lax.ppermute(value, 'tensor', [(t, t ^ 1) for t in range(8)])]
  transfers between devices with their start and end apart: 32 -> 31, of which waited for: 11 -> 12; matrix products, arithmetic and copies ran while one was open for 8% -> 8% of each run, Pallas kernels for 18% -> 18%
where the time goes in v4:
time: 233 us; the launch traced here: 232 us
  waiting for transfers between devices  67.4 us (29%)
  starting transfers between devices  54.1 us (23%)
  Pallas kernels  49.1 us (21%)
  blocking collectives  31.9 us (14%)
  local copies, waits for them, and re-layouts  18.6 us (8%)
  other arithmetic  9.89 us (4%)
    ppermute x10, waiting for transfers between devices, y_shift(): return lax.ppermute(value, 'tensor', pairs)  35.1 us
    all_to_all x2, blocking collectives, sent_to_all(): lax.all_to_all(jnp.broadcast_to(value[None], (length, *value.shape)), axi...  31.9 us
    ppermute x7, waiting for transfers between devices, z_shift(): return lax.ppermute(value, 'dp', pairs)  24 us
    pallas_call x3, Pallas kernels, project(): pl.pallas_call(functools.partial(mm_kernel, row=row, count=count, shards=...  19.5 us
    pallas_call x1, Pallas kernels, project_soon(): pl.pallas_call(functools.partial(soon_kernel, rows=rows, counts=counts, s...  16.9 us
    ppermute x10, starting transfers between devices, y_shift(): return lax.ppermute(value, 'tensor', pairs)  13.8 us
    pallas_call x2, Pallas kernels, attend(): pl.pallas_call(functools.partial(attend_kernel, seq=seq, has_in=earlier i...  12.7 us
    ppermute x7, starting transfers between devices, z_shift(): return lax.ppermute(value, 'dp', pairs)  10.6 us
  transfers between devices with their start and end apart: 31, of which 12 were waited for; matrix products, arithmetic and copies ran while one was open for 8% of the time, Pallas kernels for 18%

profile of v4, /device:TPU:1, one launch (start us, length us, event | category | flops | bytes accessed | tf_op | source)
XLA Modules:
  0.0 232.2 jit_solution(11402958041708656597)
XLA Ops:
  0.6 3.3 %collective-permute-start = (bf16[512,768]{1,0:T(8,128)(2,1)}, bf16[512,768]{1,0:T(8,128)(2,1)}, u32[]{:S(2)}, u32[]{:S(2)}) collective-permute-start(bf16[512,768]{1,0:T(8,128)(2,1)} %bitcast.72), channel_id=1, source_target_pairs={{0,16},{16,0},{32,48},{48,32},{64,80},{80,64},{96,112},{112,96},{1... | collective-permute-start | bytes 2359304 | tf_op jit(solution)/shard_map/ppermute | solution.py:47
  3.9 3.9 %collective-permute-start.3 = (bf16[512,768]{1,0:T(8,128)(2,1)}, bf16[512,768]{1,0:T(8,128)(2,1)}, u32[]{:S(2)}, u32[]{:S(2)}) collective-permute-start(bf16[512,768]{1,0:T(8,128)(2,1)} %bitcast.74), channel_id=1, source_target_pairs={{0,224},{16,240},{32,0},{48,16},{64,32},{80,48},{96,64},{112,80},{... | collective-permute-start | bytes 2359304 | tf_op jit(solution)/shard_map/ppermute | solution.py:43
  16.4 6.9 %all-to-all-start = ((bf16[16,32,1024]{2,1,0:T(8,128)(2,1)}), bf16[16,32,1024]{2,1,0:T(8,128)(2,1)}, u32[]{:S(2)}, u32[]{:S(2)}) async-start(bf16[16,32,1024]{2,1,0:T(8,128)(2,1)} %gather_fusion.1), calls=%async_computation | async-start | bytes 2097152 | tf_op jit(solution)/shard_map/all_to_all | solution.py:410
  30.1 6.4 %collective-permute-done.15.rest_15_.rest_17_ = bf16[512,1024]{1,0:T(8,128)(2,1)} collective-permute-done((bf16[512,1024]{1,0:T(8,128)(2,1)}, bf16[512,1024]{1,0:T(8,128)(2,1)}, u32[]{:S(2)}, u32[]{:S(2)}) %collective-permute-start.15) | collective-permute-done | bytes 1048608 | tf_op jit(solution)/shard_map/ppermute | solution.py:34
  40.0 10.2 %collective-permute-done.16.rest_16_.rest_18_ = bf16[512,1024]{1,0:T(8,128)(2,1)} collective-permute-done((bf16[512,1024]{1,0:T(8,128)(2,1)}, bf16[512,1024]{1,0:T(8,128)(2,1)}, u32[]{:S(2)}, u32[]{:S(2)}) %collective-permute-start.16) | collective-permute-done | bytes 1048608 | tf_op jit(solution)/shard_map/ppermute | solution.py:34
  55.8 10.4 %collective-permute-done.5.rest_6_ = bf16[512,768]{1,0:T(8,128)(2,1)} collective-permute-done((bf16[512,768]{1,0:T(8,128)(2,1)}, bf16[512,768]{1,0:T(8,128)(2,1)}, u32[]{:S(2)}, u32[]{:S(2)}) %collective-permute-start.5) | collective-permute-done | bytes 786464 | tf_op jit(solution)/shard_map/ppermute | solution.py:43
  73.9 5.3 %collective-permute-done.20.rest_19_.rest_22_ = bf16[512,1024]{1,0:T(8,128)(2,1)} collective-permute-done((bf16[512,1024]{1,0:T(8,128)(2,1)}, bf16[512,1024]{1,0:T(8,128)(2,1)}, u32[]{:S(2)}, u32[]{:S(2)}) %collective-permute-start.20) | collective-permute-done | bytes 1048608 | tf_op jit(solution)/shard_map/ppermute | solution.py:34
  79.1 2.8 %collective-permute-start.11 = (bf16[512,768]{1,0:T(8,128)(2,1)}, bf16[512,768]{1,0:T(8,128)(2,1)}, u32[]{:S(2)}, u32[]{:S(2)}) collective-permute-start(bf16[512,768]{1,0:T(8,128)(2,1)} %collective-permute-done.7.rest_8_), channel_id=1, source_target_pairs={{0,224},{16,240},{32,0},{48,16},{64,32},{80,48},{96,64},{112,80},{... | collective-permute-start | bytes 2359304 | tf_op jit(solution)/shard_map/ppermute | solution.py:43
  84.1 8.3 %collective-permute-done.9.rest_10_ = bf16[512,768]{1,0:T(8,128)(2,1)} collective-permute-done((bf16[512,768]{1,0:T(8,128)(2,1)}, bf16[512,768]{1,0:T(8,128)(2,1)}, u32[]{:S(2)}, u32[]{:S(2)}) %collective-permute-start.9) | collective-permute-done | bytes 786464 | tf_op jit(solution)/shard_map/ppermute | solution.py:43
  92.4 5.4 %collective-permute-done.11.rest_12_ = bf16[512,768]{1,0:T(8,128)(2,1)} collective-permute-done((bf16[512,768]{1,0:T(8,128)(2,1)}, bf16[512,768]{1,0:T(8,128)(2,1)}, u32[]{:S(2)}, u32[]{:S(2)}) %collective-permute-start.11) | collective-permute-done | bytes 786464 | tf_op jit(solution)/shard_map/ppermute | solution.py:43
  111.9 22.0 %all_to_all.24 = f32[8,1,1024]{2,1,0:T(1,128)S(1)} all-to-all(f32[8,1,1024]{2,1,0:T(1,128)S(1)} %broadcast_in_dim.233), channel_id=1, replica_groups=mesh['dp'=16,'tensor'=8,'mp'=2] {'tensor'}, dimensions={0} | all-to-all | bytes 65536 | tf_op jit(solution)/shard_map/all_to_all | solution.py:27
  135.3 2.7 %collective-permute-start.28 = (bf16[512,1024]{1,0:T(8,128)(2,1)}, bf16[512,1024]{1,0:T(8,128)(2,1)}, u32[]{:S(2)}, u32[]{:S(2)}) collective-permute-start(bf16[512,1024]{1,0:T(8,128)(2,1)} %collective-permute-done.23.rest_22_.rest_18_), channel_id=1, source_target_pairs={{0,2},{2,0},{4,6},{6,4},{8,10},{10,8},{12,14},{14,12},{1,3},{3,1},... | collective-permute-start | bytes 3145736 | tf_op jit(solution)/shard_map/ppermute | solution.py:38
  140.3 16.9 %project_soon.1 = (f32[512,768]{1,0:T(8,128)}, f32[512,768]{1,0:T(8,128)}) custom-call(s32[5,35]{1,0:T(8,128)S(1)} %stack.45.table_ref, f32[8,512]{1,0:T(8,128)S(1)} %get-tuple-element.41.sums_a.sums_ref, f32[8,512]{1,0:T(8,128)S(1)} %get-tuple-element.40.sums_b.sums_ref, f32[8,1024]{1,0:T(8,128)S(1)} %reshape_squeeze.7.gain_ref, ...), custom_call_target="tpu_custom_call" | custom-call | flops 6442450944 | bytes 20971520 | tf_op jit(solution)/shard_map/project_soon/pallas_call | solution.py:149
  158.2 7.4 %project.3 = bf16[512,768]{1,0:T(8,128)(2,1)S(1)} custom-call(s32[5,35]{1,0:T(8,128)S(1)} %stack.45.table_ref, f32[8,512]{1,0:T(8,128)S(1)} %get-tuple-element.41.sums_a.sums_ref, f32[8,1024]{1,0:T(8,128)S(1)} %reshape_squeeze.7.gain_ref, bf16[512,768]{1,0:T(8,128)(2,1)S(1)} %bitcast.76, bf16[512,768]{1,0:T(8,128)(2,1)} %collective-permute-done.rest_1_, ...), custom_call_target="tpu_custom_call" | custom-call | flops 3221225472 | bytes 10485760 | tf_op jit(solution)/shard_map/project/pallas_call | solution.py:228
  166.5 6.3 %all-to-all-start.2 = ((bf16[16,32,768]{2,1,0:T(8,128)(2,1)}), bf16[16,32,768]{2,1,0:T(8,128)(2,1)}, u32[]{:S(2)}, u32[]{:S(2)}) async-start(bf16[16,32,768]{2,1,0:T(8,128)(2,1)} %bitcast.79), calls=%async_computation.2 | async-start | bytes 1572864 | tf_op jit(solution)/shard_map/all_to_all | solution.py:507
  172.8 3.2 %collective-permute-start.25 = (bf16[512,1024]{1,0:T(8,128)(2,1)}, bf16[512,1024]{1,0:T(8,128)(2,1)}, u32[]{:S(2)}, u32[]{:S(2)}) collective-permute-start(bf16[512,1024]{1,0:T(8,128)(2,1)} %collective-permute-done.23.rest_22_.rest_18_), channel_id=1, source_target_pairs={{0,12},{2,14},{4,0},{6,2},{8,4},{10,6},{12,8},{14,10},{1,13},{3,15... | collective-permute-start | bytes 3145736 | tf_op jit(solution)/shard_map/ppermute | solution.py:34
  176.1 7.9 %collective-permute-done.28.rest_21_ = bf16[512,1024]{1,0:T(8,128)(2,1)} collective-permute-done((bf16[512,1024]{1,0:T(8,128)(2,1)}, bf16[512,1024]{1,0:T(8,128)(2,1)}, u32[]{:S(2)}, u32[]{:S(2)}) %collective-permute-start.28) | collective-permute-done | bytes 1048608 | tf_op jit(solution)/shard_map/ppermute | solution.py:38
  186.2 6.5 %project.4.rest_18_ = f32[512,768]{1,0:T(8,128)} custom-call(s32[5,35]{1,0:T(8,128)S(1)} %stack.45.table_ref, f32[8,512]{1,0:T(8,128)S(1)} %get-tuple-element.40.sums_b.sums_ref, f32[8,1024]{1,0:T(8,128)S(1)} %reshape_squeeze.7.gain_ref, bf16[512,768]{1,0:T(8,128)(2,1)S(1)} %bitcast.77, bf16[512,768]{1,0:T(8,128)(2,1)} %collective-permute-done.rest_1_, ...), custom_call_target="tpu_custom_call" | custom-call | flops 3221225472 | bytes 10485760 | tf_op jit(solution)/shard_map/project/pallas_call | solution.py:228
  192.8 5.8 %collective-permute-done.25.rest_16_ = bf16[512,1024]{1,0:T(8,128)(2,1)} collective-permute-done((bf16[512,1024]{1,0:T(8,128)(2,1)}, bf16[512,1024]{1,0:T(8,128)(2,1)}, u32[]{:S(2)}, u32[]{:S(2)}) %collective-permute-start.25) | collective-permute-done | bytes 1048608 | tf_op jit(solution)/shard_map/ppermute | solution.py:34
  198.7 3.1 %collective-permute-done.27.rest_17_ = bf16[512,1024]{1,0:T(8,128)(2,1)} collective-permute-done((bf16[512,1024]{1,0:T(8,128)(2,1)}, bf16[512,1024]{1,0:T(8,128)(2,1)}, u32[]{:S(2)}, u32[]{:S(2)}) %collective-permute-start.27) | collective-permute-done | bytes 1048608 | tf_op jit(solution)/shard_map/ppermute | solution.py:34
  201.8 5.6 %project.5 = bf16[512,768]{1,0:T(8,128)(2,1)S(1)} custom-call(s32[5,35]{1,0:T(8,128)S(1)} %stack.45.table_ref, f32[8,512]{1,0:T(8,128)S(1)} %get-tuple-element.40.sums_b.sums_ref, f32[8,1024]{1,0:T(8,128)S(1)} %reshape_squeeze.7.gain_ref, bf16[512,768]{1,0:T(8,128)(2,1)S(1)} %bitcast.78, bf16[512,768]{1,0:T(8,128)(2,1)} %collective-permute-done.rest_1_, ...), custom_call_target="tpu_custom_call" | custom-call | flops 1610612736 | bytes 5242880 | tf_op jit(solution)/shard_map/project/pallas_call | solution.py:228
  207.4 6.4 %attend.2 = (bf16[32,32,512]{2,1,0:T(8,128)(2,1)}, f32[32,128]{1,0:T(8,128)S(1)}) custom-call(s32[3,16]{1,0:T(4,128)S(1)} %get-tuple-element.18.meta_ref, s32[4]{0:T(128)S(1)} %copy-done.14, bf16[16,32,768]{2,1,0:T(8,128)(2,1)S(1)} %bitcast.82, bf16[4,768,256]{2,1,0:T(8,128)(2,1)S(1)} %bitcast.80, f32[4,128]{1,0:T(4,128)S(1)} %bitcast.83), custom_call_target="tpu_custom_call" | custom-call | flops 805306368 | bytes 3407872 | tf_op jit(solution)/shard_map/attend/pallas_call | solution.py:356
  215.2 6.3 %attend.3 = (bf16[32,32,512]{2,1,0:T(8,128)(2,1)}, f32[32,128]{1,0:T(8,128)S(1)}) custom-call(s32[3,16]{1,0:T(4,128)S(1)} %get-tuple-element.13.meta_ref, s32[4]{0:T(128)S(1)} %copy-done.14, bf16[16,32,768]{2,1,0:T(8,128)(2,1)} %all-to-all-done.2.rows_hbm, bf16[4,768,256]{2,1,0:T(8,128)(2,1)S(1)} %bitcast.81, ...), custom_call_target="tpu_custom_call", output_to_operand_aliasing={{0}: (5, {})} | custom-call | flops 805306368 | bytes 3407872 | tf_op jit(solution)/shard_map/attend/pallas_call | solution.py:356
  221.7 9.9 %all_to_all.25 = f32[16,4,8]{2,1,0:T(4,128)S(1)} all-to-all(f32[16,4,8]{2,1,0:T(4,128)S(1)} %broadcast_in_dim.234), channel_id=1, replica_groups=mesh['dp'=16,'tensor'=8,'mp'=2] {'tensor','mp'}, dimensions={0} | all-to-all | bytes 4096 | tf_op jit(solution)/shard_map/all_to_all | solution.py:27
  (191 shorter events, 58.1 us)
Async XLA Ops:
  0.6 24.7 %collective-permute-start = (bf16[512,768]{1,0:T(8,128)(2,1)}, bf16[512,768]{1,0:T(8,128)(2,1)}, u32[]{:S(2)}, u32[]{:S(2)}) collective-permute-start(bf16[512,768]{1,0:T(8,128)(2,1)} %bitcast.72), channel_id=1, source_target_pairs={{0,16},{16,0},{32,48},{48,32},{64,80},{80,64},{96,112},{112,96},{1... | collective-permute-start | bytes 2359304 | tf_op jit(solution)/shard_map/ppermute | solution.py:47
  3.9 24.1 %collective-permute-start.1 = (bf16[512,768]{1,0:T(8,128)(2,1)}, bf16[512,768]{1,0:T(8,128)(2,1)}, u32[]{:S(2)}, u32[]{:S(2)}) collective-permute-start(bf16[512,768]{1,0:T(8,128)(2,1)} %bitcast.73), channel_id=1, source_target_pairs={{0,32},{16,48},{32,64},{48,80},{64,96},{80,112},{96,128},{112,144}... | collective-permute-start | bytes 2359304 | tf_op jit(solution)/shard_map/ppermute | solution.py:43
  3.9 24.6 %collective-permute-start.3 = (bf16[512,768]{1,0:T(8,128)(2,1)}, bf16[512,768]{1,0:T(8,128)(2,1)}, u32[]{:S(2)}, u32[]{:S(2)}) collective-permute-start(bf16[512,768]{1,0:T(8,128)(2,1)} %bitcast.74), channel_id=1, source_target_pairs={{0,224},{16,240},{32,0},{48,16},{64,32},{80,48},{96,64},{112,80},{... | collective-permute-start | bytes 2359304 | tf_op jit(solution)/shard_map/ppermute | solution.py:43
  10.6 25.9 %collective-permute-start.15 = (bf16[512,1024]{1,0:T(8,128)(2,1)}, bf16[512,1024]{1,0:T(8,128)(2,1)}, u32[]{:S(2)}, u32[]{:S(2)}) collective-permute-start(bf16[512,1024]{1,0:T(8,128)(2,1)} %bitcast.85), channel_id=1, source_target_pairs={{0,4},{2,6},{4,8},{6,10},{8,12},{10,14},{12,0},{14,2},{1,5},{3,7},... | collective-permute-start | bytes 3145736 | tf_op jit(solution)/shard_map/ppermute | solution.py:34
  11.9 26.7 %collective-permute-start.17 = (bf16[512,1024]{1,0:T(8,128)(2,1)}, bf16[512,1024]{1,0:T(8,128)(2,1)}, u32[]{:S(2)}, u32[]{:S(2)}) collective-permute-start(bf16[512,1024]{1,0:T(8,128)(2,1)} %bitcast.86), channel_id=1, source_target_pairs={{0,2},{2,0},{4,6},{6,4},{8,10},{10,8},{12,14},{14,12},{1,3},{3,1},... | collective-permute-start | bytes 3145736 | tf_op jit(solution)/shard_map/ppermute | solution.py:38
  16.4 52.4 %all-to-all-start = ((bf16[16,32,1024]{2,1,0:T(8,128)(2,1)}), bf16[16,32,1024]{2,1,0:T(8,128)(2,1)}, u32[]{:S(2)}, u32[]{:S(2)}) async-start(bf16[16,32,1024]{2,1,0:T(8,128)(2,1)} %gather_fusion.1), calls=%async_computation | async-start | bytes 2097152 | tf_op jit(solution)/shard_map/all_to_all | solution.py:410
  25.3 24.9 %collective-permute-start.16 = (bf16[512,1024]{1,0:T(8,128)(2,1)}, bf16[512,1024]{1,0:T(8,128)(2,1)}, u32[]{:S(2)}, u32[]{:S(2)}) collective-permute-start(bf16[512,1024]{1,0:T(8,128)(2,1)} %bitcast.87), channel_id=1, source_target_pairs={{0,12},{2,14},{4,0},{6,2},{8,4},{10,6},{12,8},{14,10},{1,13},{3,15... | collective-permute-start | bytes 3145736 | tf_op jit(solution)/shard_map/ppermute | solution.py:34
  28.5 37.6 %collective-permute-start.5 = (bf16[512,768]{1,0:T(8,128)(2,1)}, bf16[512,768]{1,0:T(8,128)(2,1)}, u32[]{:S(2)}, u32[]{:S(2)}) collective-permute-start(bf16[512,768]{1,0:T(8,128)(2,1)} %collective-permute-done.1.rest_2_), channel_id=1, source_target_pairs={{0,32},{16,48},{32,64},{48,80},{64,96},{80,112},{96,128},{112,144}... | collective-permute-start | bytes 2359304 | tf_op jit(solution)/shard_map/ppermute | solution.py:43
  36.5 30.6 %collective-permute-start.7 = (bf16[512,768]{1,0:T(8,128)(2,1)}, bf16[512,768]{1,0:T(8,128)(2,1)}, u32[]{:S(2)}, u32[]{:S(2)}) collective-permute-start(bf16[512,768]{1,0:T(8,128)(2,1)} %collective-permute-done.3.rest_4_), channel_id=1, source_target_pairs={{0,224},{16,240},{32,0},{48,16},{64,32},{80,48},{96,64},{112,80},{... | collective-permute-start | bytes 2359304 | tf_op jit(solution)/shard_map/ppermute | solution.py:43
  38.6 34.2 %collective-permute-start.19 = (bf16[512,1024]{1,0:T(8,128)(2,1)}, bf16[512,1024]{1,0:T(8,128)(2,1)}, u32[]{:S(2)}, u32[]{:S(2)}) collective-permute-start(bf16[512,1024]{1,0:T(8,128)(2,1)} %collective-permute-done.17.rest_17_.rest_19_), channel_id=1, source_target_pairs={{0,12},{2,14},{4,0},{6,2},{8,4},{10,6},{12,8},{14,10},{1,13},{3,15... | collective-permute-start | bytes 3145736 | tf_op jit(solution)/shard_map/ppermute | solution.py:34
  52.9 26.2 %collective-permute-start.20 = (bf16[512,1024]{1,0:T(8,128)(2,1)}, bf16[512,1024]{1,0:T(8,128)(2,1)}, u32[]{:S(2)}, u32[]{:S(2)}) collective-permute-start(bf16[512,1024]{1,0:T(8,128)(2,1)} %collective-permute-done.15.rest_15_.rest_17_), channel_id=1, source_target_pairs={{0,4},{2,6},{4,8},{6,10},{8,12},{10,14},{12,0},{14,2},{1,5},{3,7},... | collective-permute-start | bytes 3145736 | tf_op jit(solution)/shard_map/ppermute | solution.py:34
  68.7 32.9 %collective-permute-start.22 = (bf16[512,1024]{1,0:T(8,128)(2,1)}, bf16[512,1024]{1,0:T(8,128)(2,1)}, u32[]{:S(2)}, u32[]{:S(2)}) collective-permute-start(bf16[512,1024]{1,0:T(8,128)(2,1)} %bitcast.34.rest_20_.rest_16_), channel_id=1, source_target_pairs={{0,4},{2,6},{4,8},{6,10},{8,12},{10,14},{12,0},{14,2},{1,5},{3,7},... | collective-permute-start | bytes 3145736 | tf_op jit(solution)/shard_map/ppermute | solution.py:34
  81.9 25.6 %collective-permute-start.23 = (bf16[512,1024]{1,0:T(8,128)(2,1)}, bf16[512,1024]{1,0:T(8,128)(2,1)}, u32[]{:S(2)}, u32[]{:S(2)}) collective-permute-start(bf16[512,1024]{1,0:T(8,128)(2,1)} %bitcast.34.rest_20_.rest_16_), channel_id=1, source_target_pairs={{0,12},{2,14},{4,0},{6,2},{8,4},{10,6},{12,8},{14,10},{1,13},{3,15... | collective-permute-start | bytes 3145736 | tf_op jit(solution)/shard_map/ppermute | solution.py:34
  83.3 24.7 %collective-permute-start.24 = (bf16[512,1024]{1,0:T(8,128)(2,1)}, bf16[512,1024]{1,0:T(8,128)(2,1)}, u32[]{:S(2)}, u32[]{:S(2)}) collective-permute-start(bf16[512,1024]{1,0:T(8,128)(2,1)} %bitcast.34.rest_20_.rest_16_), channel_id=1, source_target_pairs={{0,2},{2,0},{4,6},{6,4},{8,10},{10,8},{12,14},{14,12},{1,3},{3,1},... | collective-permute-start | bytes 3145736 | tf_op jit(solution)/shard_map/ppermute | solution.py:38
  92.3 41.5 %collective-permute-start.13 = (bf16[512,768]{1,0:T(8,128)(2,1)}, bf16[512,768]{1,0:T(8,128)(2,1)}, u32[]{:S(2)}, u32[]{:S(2)}) collective-permute-start(bf16[512,768]{1,0:T(8,128)(2,1)} %collective-permute-done.9.rest_10_), channel_id=1, source_target_pairs={{0,32},{16,48},{32,64},{48,80},{64,96},{80,112},{96,128},{112,144}... | collective-permute-start | bytes 2359304 | tf_op jit(solution)/shard_map/ppermute | solution.py:43
  97.8 37.2 %collective-permute-start.10 = (bf16[512,768]{1,0:T(8,128)(2,1)}, bf16[512,768]{1,0:T(8,128)(2,1)}, u32[]{:S(2)}, u32[]{:S(2)}) collective-permute-start(bf16[512,768]{1,0:T(8,128)(2,1)} %collective-permute-done.9.rest_10_), channel_id=1, source_target_pairs={{0,16},{16,0},{32,48},{48,32},{64,80},{80,64},{96,112},{112,96},{1... | collective-permute-start | bytes 2359304 | tf_op jit(solution)/shard_map/ppermute | solution.py:47
  101.6 33.7 %collective-permute-start.12 = (bf16[512,768]{1,0:T(8,128)(2,1)}, bf16[512,768]{1,0:T(8,128)(2,1)}, u32[]{:S(2)}, u32[]{:S(2)}) collective-permute-start(bf16[512,768]{1,0:T(8,128)(2,1)} %collective-permute-done.11.rest_12_), channel_id=1, source_target_pairs={{0,16},{16,0},{32,48},{48,32},{64,80},{80,64},{96,112},{112,96},{1... | collective-permute-start | bytes 2359304 | tf_op jit(solution)/shard_map/ppermute | solution.py:47
  107.6 49.7 %collective-permute-start.18 = (bf16[512,1024]{1,0:T(8,128)(2,1)}, bf16[512,1024]{1,0:T(8,128)(2,1)}, u32[]{:S(2)}, u32[]{:S(2)}) collective-permute-start(bf16[512,1024]{1,0:T(8,128)(2,1)} %collective-permute-done.17.rest_17_.rest_19_), channel_id=1, source_target_pairs={{0,4},{2,6},{4,8},{6,10},{8,12},{10,14},{12,0},{14,2},{1,5},{3,7},... | collective-permute-start | bytes 3145736 | tf_op jit(solution)/shard_map/ppermute | solution.py:34
  108.0 49.3 %collective-permute-start.21 = (bf16[512,1024]{1,0:T(8,128)(2,1)}, bf16[512,1024]{1,0:T(8,128)(2,1)}, u32[]{:S(2)}, u32[]{:S(2)}) collective-permute-start(bf16[512,1024]{1,0:T(8,128)(2,1)} %collective-permute-done.19.rest_18_.rest_21_), channel_id=1, source_target_pairs={{0,12},{2,14},{4,0},{6,2},{8,4},{10,6},{12,8},{14,10},{1,13},{3,15... | collective-permute-start | bytes 3145736 | tf_op jit(solution)/shard_map/ppermute | solution.py:34
  135.1 41.0 %collective-permute-start.26 = (bf16[512,1024]{1,0:T(8,128)(2,1)}, bf16[512,1024]{1,0:T(8,128)(2,1)}, u32[]{:S(2)}, u32[]{:S(2)}) collective-permute-start(bf16[512,1024]{1,0:T(8,128)(2,1)} %collective-permute-done.22.rest_21_.rest_17_), channel_id=1, source_target_pairs={{0,2},{2,0},{4,6},{6,4},{8,10},{10,8},{12,14},{14,12},{1,3},{3,1},... | collective-permute-start | bytes 3145736 | tf_op jit(solution)/shard_map/ppermute | solution.py:38
  135.3 48.7 %collective-permute-start.28 = (bf16[512,1024]{1,0:T(8,128)(2,1)}, bf16[512,1024]{1,0:T(8,128)(2,1)}, u32[]{:S(2)}, u32[]{:S(2)}) collective-permute-start(bf16[512,1024]{1,0:T(8,128)(2,1)} %collective-permute-done.23.rest_22_.rest_18_), channel_id=1, source_target_pairs={{0,2},{2,0},{4,6},{6,4},{8,10},{10,8},{12,14},{14,12},{1,3},{3,1},... | collective-permute-start | bytes 3145736 | tf_op jit(solution)/shard_map/ppermute | solution.py:38
  166.5 47.3 %all-to-all-start.2 = ((bf16[16,32,768]{2,1,0:T(8,128)(2,1)}), bf16[16,32,768]{2,1,0:T(8,128)(2,1)}, u32[]{:S(2)}, u32[]{:S(2)}) async-start(bf16[16,32,768]{2,1,0:T(8,128)(2,1)} %bitcast.79), calls=%async_computation.2 | async-start | bytes 1572864 | tf_op jit(solution)/shard_map/all_to_all | solution.py:507
  172.8 25.9 %collective-permute-start.25 = (bf16[512,1024]{1,0:T(8,128)(2,1)}, bf16[512,1024]{1,0:T(8,128)(2,1)}, u32[]{:S(2)}, u32[]{:S(2)}) collective-permute-start(bf16[512,1024]{1,0:T(8,128)(2,1)} %collective-permute-done.23.rest_22_.rest_18_), channel_id=1, source_target_pairs={{0,12},{2,14},{4,0},{6,2},{8,4},{10,6},{12,8},{14,10},{1,13},{3,15... | collective-permute-start | bytes 3145736 | tf_op jit(solution)/shard_map/ppermute | solution.py:34
  176.1 25.7 %collective-permute-start.27 = (bf16[512,1024]{1,0:T(8,128)(2,1)}, bf16[512,1024]{1,0:T(8,128)(2,1)}, u32[]{:S(2)}, u32[]{:S(2)}) collective-permute-start(bf16[512,1024]{1,0:T(8,128)(2,1)} %collective-permute-done.26.rest_20_), channel_id=1, source_target_pairs={{0,4},{2,6},{4,8},{6,10},{8,12},{10,14},{12,0},{14,2},{1,5},{3,7},... | collective-permute-start | bytes 3145736 | tf_op jit(solution)/shard_map/ppermute | solution.py:34
  (37 other events, 556.5 us)
